TPU v7x, 32 devices: a whole 2x2x4 slice. The times are simulated.
32 devices in a mesh: parts: 2 (over y), row: 4 (over z), col: 4 (over x, core).
Axes of the slice: x: 2, y: 2, z: 4, core: 2. Of those that a mesh axis runs over, the one named last changes fastest.
Arguments:
- single: bfloat16 [8, 1024, 768], P(None, ('parts', 'row'), 'col'), parts along dimension 1, may hold values from -6 to 6
- pair_act: bfloat16 [1024, 512, 128], P(('parts', 'row'), 'col'), parts along dimension 0, may hold values from -6 to 6
- token_mask: int32 [1024], P(('parts', 'row')), parts along dimension 0, may hold values 0 or 1
- atom_feats: bfloat16 [8192, 128], P(('parts', 'row', 'col')), parts along dimension 0, may hold values from -6 to 6
- atom_token: int32 [8192], P(('parts', 'row', 'col')), parts along dimension 0, may hold values from 0 to 127, as said below
- atom_count: int32 [32], P(('parts', 'row', 'col')), parts along dimension 0, may hold values from 32 to 256, as said below
- atom_weight: bfloat16 [128, 768], P(None, 'col'), may hold values from -0.5 to 0.5
- bias_weight: bfloat16 [128, 2, 16], replicated, may hold values from -16 to 16
- qkvg_weight: bfloat16 [2, 4, 768, 768], P(None, None, 'col'), may hold values from -0.21875 to 0.21875
- out_weight: bfloat16 [2, 768, 768], P(None, 'col'), may hold values from -0.21875 to 0.21875
Outputs:
- updated: bfloat16 [8, 1024, 768], P(None, ('parts', 'row'), 'col'), parts along dimension 1
There are 2 independent parts, one for each index of `parts`. A program takes and returns all parts, laid end to end along the dimension named above; an argument that names none is the same for every part. Nothing has to cross between parts.
Inputs may be any that keep to these rules, and one draw needn't show every extreme that they name: `atom_token`: slots of a device hold atoms of the 128 tokens of that device's row block, numbered within the block; every token owns at least one live slot. The first atom_count slots of a device are live, the others are padding; in every draw some device has all 256 slots live.
All inputs are finite; a program needn't handle non-finite values. No bound on the sum of `token_mask` on one device may be relied on, other than what follows from the above.
Results may differ from a plain program's by a relative error of at most 0.014.
The roundings to bfloat16 on the way count: a program that leaves them out, or rounds other values in their place, can miss the bound.
Values may be sent and summed in bfloat16 or wider, within the bound.
A program may use at most 64 MiB of HBM per device.

v0:
```python
import math

import jax
import jax.numpy as jnp
from jax import lax
from jax.experimental import pallas as pl
from jax.experimental.pallas import tpu as pltpu
from jax.sharding import PartitionSpec as P

HEAD_DIM = 48
LAYERS = 2


EPS = 1e-05
MASKED = -1000000000.0
START_LOW = -1e30


def layer_norm(values):
    average = jnp.mean(values, axis=-1, keepdims=True)
    centered = values - average
    variance = jnp.mean(centered * centered, axis=-1, keepdims=True)
    return centered * lax.rsqrt(variance + EPS)


def per_device(
    single,
    pair_act,
    token_mask,
    atom_feats,
    atom_token,
    atom_count,
    atom_weight,
    bias_weight,
    qkvg_weight,
    out_weight,
):
    tok_rows = single.shape[1]
    sample_count = single.shape[0]
    slot_ids = jnp.arange(atom_feats.shape[0], dtype=jnp.int32)
    live_slots = slot_ids < atom_count[0]
    token_ids = jnp.arange(tok_rows, dtype=jnp.int32)
    owner_match = (token_ids[:, None] == atom_token[None, :]) & live_slots[None, :]
    owners = owner_match.astype(jnp.float32)
    counts = jnp.sum(owners, axis=1)
    atom_sums = jnp.dot(
        owner_match.astype(jnp.bfloat16), atom_feats, preferred_element_type=jnp.float32
    )
    sum_total, count_total = (
        lax.psum(atom_sums.astype(jnp.bfloat16), "col").astype(jnp.float32),
        lax.psum(counts[:, None].astype(jnp.bfloat16), "col").astype(jnp.float32),
    )
    pooled = (
        jnp.dot(sum_total, atom_weight.astype(jnp.float32), precision=lax.Precision.HIGHEST)
        / count_total
    )
    stream = (single.astype(jnp.float32) + pooled[None]).astype(jnp.bfloat16)
    pair_normed = layer_norm(pair_act.astype(jnp.float32)).astype(jnp.bfloat16)
    biases = jnp.einsum(
        "ijc,clh->lhij", pair_normed, bias_weight, preferred_element_type=jnp.float32
    ).astype(jnp.bfloat16)
    live_keys = (token_mask > 0).astype(jnp.bfloat16)[None, :]
    score_scale = 1.0 / math.sqrt(HEAD_DIM)
    for layer_idx in range(LAYERS):
        spread = lax.all_to_all(biases[layer_idx], "col", split_axis=0, concat_axis=2, tiled=True)
        gathered = lax.all_gather(stream, "col", axis=2, tiled=True)
        normed = layer_norm(gathered.astype(jnp.float32)).astype(jnp.bfloat16)
        projected = jnp.einsum(
            "std,fed->fste", normed, qkvg_weight[layer_idx], preferred_element_type=jnp.float32
        )
        head_width = projected.shape[3]
        heads_here = head_width // HEAD_DIM
        queries = (
            projected[0].astype(jnp.bfloat16).reshape(sample_count, tok_rows, heads_here, HEAD_DIM)
        )
        key_rows = projected[1].astype(jnp.bfloat16)
        value_rows = projected[2].astype(jnp.bfloat16)
        gating = jax.nn.sigmoid(projected[3])

        def attend(running, incoming, offset, queries=queries, spread=spread):
            top_old, summed_old, acc_old = running
            keys_in, values_in, live_in = incoming
            key_count = keys_in.shape[1]
            keys_heads = keys_in.reshape(sample_count, key_count, heads_here, HEAD_DIM)
            values_heads = values_in.reshape(sample_count, key_count, heads_here, HEAD_DIM)
            scores = (
                jnp.einsum(
                    "sqhd,skhd->shqk", queries, keys_heads, preferred_element_type=jnp.float32
                )
                * score_scale
            )
            scores = scores + spread.astype(jnp.float32)[None]
            scores = jnp.where(live_in[0][None, None, None, :] > 0, scores, MASKED)
            top_new = jnp.maximum(top_old, jnp.max(scores, axis=-1))
            exponent = jnp.exp(scores - top_new[..., None])
            summed_new = jnp.sum(exponent, axis=-1)
            weights = exponent.astype(jnp.bfloat16)
            acc_new = jnp.einsum(
                "shqk,skhd->shqd", weights, values_heads, preferred_element_type=jnp.float32
            )
            return (top_new, summed_new, acc_new)

        start_state = (
            jnp.full((sample_count, heads_here, tok_rows), START_LOW, jnp.float32),
            jnp.zeros((sample_count, heads_here, tok_rows), jnp.float32),
            jnp.zeros((sample_count, heads_here, tok_rows, HEAD_DIM), jnp.float32),
        )
        top_end, summed_end, acc_end = attend(
            start_state,
            (
                lax.all_gather(key_rows, "row", axis=1, tiled=True),
                lax.all_gather(value_rows, "row", axis=1, tiled=True),
                lax.all_gather(live_keys, "row", axis=1, tiled=True),
            ),
            jnp.int32(0),
        )
        attended = acc_end / summed_end[..., None]
        attended = attended.transpose(0, 2, 1, 3).reshape(sample_count, tok_rows, head_width)
        gated = (gating * attended).astype(jnp.bfloat16)
        out_rows = out_weight[layer_idx]

        def project(summed, incoming, offset, out_rows=out_rows):
            return jnp.einsum("std,ed->ste", incoming, out_rows, preferred_element_type=jnp.float32)

        zero_update = jnp.zeros((sample_count, tok_rows, out_rows.shape[0]), jnp.float32)
        update = project(
            zero_update, lax.all_gather(gated, "col", axis=2, tiled=True), jnp.int32(0)
        )
        stream = (stream.astype(jnp.float32) + update).astype(jnp.bfloat16)
    return stream


MESH = pl.DeviceIdType.MESH
NT = (((1,), (1,)), ((), ()))


def remote(src, dst, send_sem, recv_sem, row, col):
    return pltpu.make_async_remote_copy(
        src_ref=src,
        dst_ref=dst,
        send_sem=send_sem,
        recv_sem=recv_sem,
        device_id={"row": row, "col": col},
        device_id_type=MESH,
    )


def fused(
    rows,
    cols,
    bias,
    single,
    feats,
    slot_token,
    slot_count,
    atom_weight,
    mask,
    qkvg,
    out_w,
    out,
    spread,
    normed,
    out_full,
    stream,
    parts_buf,
    stream_send,
    stream_recv,
    mask_buf,
    queries,
    keys,
    values,
    gates,
    gated_send,
    gated_recv,
    final_send,
    part_sems,
    mask_sems,
    a2a_sems,
    ring_sems,
    out_w_sems,
    in_sems,
    ag_sems,
    gated_sems,
    end_sems,
):
    r = lax.axis_index("row")
    c = lax.axis_index("col")
    own = single.shape[0] // rows
    tokens = single.shape[2]
    width = single.shape[1]
    heads = width // HEAD_DIM
    sibling = c + 1 - 2 * lax.rem(c, 2)
    across = lax.rem(c + 2, cols)
    far = lax.rem(sibling + 2, cols)
    on_diag = r == c

    barrier = pltpu.get_barrier_semaphore()
    for dr in range(rows):
        for dc in range(cols):
            if dr or dc:
                pl.semaphore_signal(
                    barrier,
                    inc=1,
                    device_id={"row": lax.rem(r + dr, rows), "col": lax.rem(c + dc, cols)},
                    device_id_type=MESH,
                )
    pl.semaphore_wait(barrier, rows * cols - 1)

    sent = []

    def col_of(d):
        return lax.rem(c + d, cols)

    def bias_exchange(l):
        for d in range(1, cols):
            to = col_of(d)
            desc = remote(
                bias.at[l, to],
                spread.at[l, r, c],
                a2a_sems.at[0, l, d],
                a2a_sems.at[1, l, d],
                r,
                to,
            )
            desc.start()
            sent.append(desc)
        spread[l, r, c] = bias[l, c]

    def bias_exchange_wait(l):
        for d in range(1, cols):
            frm = col_of(cols - d)
            remote(
                bias.at[l, frm],
                spread.at[l, r, frm],
                a2a_sems.at[0, l, d],
                a2a_sems.at[1, l, d],
                r,
                frm,
            ).wait_recv()

    def ring_desc(l, right, step, block):
        side = 0 if right else 1
        to = r + 1 if right else r - 1
        return remote(
            spread.at[l, block],
            spread.at[l, block],
            ring_sems.at[0, l, side, step],
            ring_sems.at[1, l, side, step],
            to,
            c,
        )

    def ring_send(l, step):
        @pl.when((r + 1 < rows) & (r - step >= 0))
        def _():
            ring_desc(l, True, step, r - step).start()

        @pl.when((r - 1 >= 0) & (r + step < rows))
        def _():
            ring_desc(l, False, step, r + step).start()

    def ring_sent(l, step):
        @pl.when((r + 1 < rows) & (r - step >= 0))
        def _():
            ring_desc(l, True, step, r - step).wait_send()

        @pl.when((r - 1 >= 0) & (r + step < rows))
        def _():
            ring_desc(l, False, step, r + step).wait_send()

    def advance(l, step):
        @pl.when(r - 1 - step >= 0)
        def _():
            block = r - 1 - step
            remote(
                spread.at[l, block],
                spread.at[l, block],
                ring_sems.at[0, l, 0, step],
                ring_sems.at[1, l, 0, step],
                r - 1,
                c,
            ).wait_recv()

        @pl.when((r - 1 - step >= 0) & (r + 1 < rows) & (step + 1 < rows - 1))
        def _():
            ring_desc(l, True, step + 1, r - step - 1).start()

        @pl.when(r + 1 + step < rows)
        def _():
            block = r + 1 + step
            remote(
                spread.at[l, block],
                spread.at[l, block],
                ring_sems.at[0, l, 1, step],
                ring_sems.at[1, l, 1, step],
                r + 1,
                c,
            ).wait_recv()

        @pl.when((r + 1 + step < rows) & (r - 1 >= 0) & (step + 1 < rows - 1))
        def _():
            ring_desc(l, False, step + 1, r + step + 1).start()

    for d in range(1, rows):
        to = lax.rem(r + d, rows)
        desc = remote(mask, mask_buf.at[r], mask_sems.at[0, d], mask_sems.at[1, d], to, c)
        desc.start()
        sent.append(desc)
    mask_buf[r] = mask[...]

    slots = feats.shape[0]
    token_ids = lax.broadcasted_iota(jnp.int32, (tokens, slots), 0)
    slot_ids = lax.broadcasted_iota(jnp.int32, (tokens, slots), 1)
    match = (token_ids == slot_token[...]) & (slot_ids < slot_count[...])
    owners = jnp.where(match, 1.0, 0.0).astype(jnp.bfloat16)
    parts_buf[c, 0:tokens] = jnp.dot(
        owners, feats[...], preferred_element_type=jnp.float32
    ).astype(jnp.bfloat16)
    parts_buf[c, tokens : tokens + 16] = lax.dot_general(
        jnp.ones((16, slots), jnp.bfloat16), owners, NT, preferred_element_type=jnp.float32
    ).astype(jnp.bfloat16)
    for d in range(1, cols):
        desc = remote(
            parts_buf.at[c], parts_buf.at[c], part_sems.at[0, d], part_sems.at[1, d], r, col_of(d)
        )
        desc.start()
        sent.append(desc)
    bias_exchange(0)
    for d in range(1, cols):
        frm = col_of(cols - d)
        remote(
            parts_buf.at[frm], parts_buf.at[frm], part_sems.at[0, d], part_sems.at[1, d], r, frm
        ).wait_recv()
    total = jnp.zeros((width, tokens), jnp.float32)
    count_row = jnp.zeros((1, tokens), jnp.float32)
    for k in range(cols):
        total = total + lax.dot_general(
            atom_weight[...], parts_buf[k, 0:tokens], NT, preferred_element_type=jnp.float32
        )
        count_row = count_row + parts_buf[k, tokens : tokens + 16].astype(jnp.float32)[0:1]
    pooled = total / count_row
    for s in range(single.shape[0]):
        stream_send[s] = (single[s].astype(jnp.float32) + pooled).astype(jnp.bfloat16)
    for d in range(rows):
        to = lax.rem(r + d, rows)
        piece = stream_send.at[pl.ds(to * own, own)]
        if d == 0:

            @pl.when(on_diag)
            def _():
                stream_recv[c] = stream_send[pl.ds(r * own, own)]

            @pl.when(jnp.logical_not(on_diag))
            def _(piece=piece, to=to):
                remote(piece, stream_recv.at[c], in_sems.at[0, 0], in_sems.at[1, c], to, r).start()

        else:
            desc = remote(piece, stream_recv.at[c], in_sems.at[0, d], in_sems.at[1, c], to, r)
            desc.start()
            sent.append(desc)

    bias_exchange_wait(0)
    ring_send(0, 0)

    def out_w_send(l):
        for kind, to in ((0, sibling), (1, across)):
            desc = remote(
                out_w.at[l],
                out_full.at[c, l],
                out_w_sems.at[0, l, kind],
                out_w_sems.at[1, l, kind],
                r,
                to,
            )
            desc.start()
            sent.append(desc)
        out_full[c, l] = out_w[l]

    def out_w_arrived(l, kind, block):
        remote(
            out_w.at[l],
            out_full.at[block, l],
            out_w_sems.at[0, l, kind],
            out_w_sems.at[1, l, kind],
            r,
            sibling,
        ).wait_recv()

    for f in range(cols):

        @pl.when(jnp.logical_not(on_diag & (c == f)))
        def _(f=f):
            remote(
                stream_recv.at[f],
                stream_recv.at[f],
                in_sems.at[0, 0],
                in_sems.at[1, f],
                c,
                f,
            ).wait_recv()

    def send_normed(l, s, here):
        average = jnp.mean(here, axis=0, keepdims=True)
        centered = here - average
        variance = jnp.mean(centered * centered, axis=0, keepdims=True)
        normed[l, s, c] = (centered * lax.rsqrt(variance + EPS)).astype(jnp.bfloat16)
        for kind, to in ((0, sibling), (1, across)):
            desc = remote(
                normed.at[l, s, c],
                normed.at[l, s, c],
                ag_sems.at[0, l, s, kind],
                ag_sems.at[1, l, s, kind],
                r,
                to,
            )
            desc.start()
            sent.append(desc)

    def forward_normed(l, s):
        remote(
            normed.at[l, s, across],
            normed.at[l, s, across],
            ag_sems.at[0, l, s, 1],
            ag_sems.at[1, l, s, 1],
            r,
            across,
        ).wait_recv()
        desc = remote(
            normed.at[l, s, across],
            normed.at[l, s, across],
            ag_sems.at[0, l, s, 2],
            ag_sems.at[1, l, s, 2],
            r,
            sibling,
        )
        desc.start()
        sent.append(desc)

    def project(l, s):
        for kind, block in ((0, sibling), (2, far)):
            remote(
                normed.at[l, s, block],
                normed.at[l, s, block],
                ag_sems.at[0, l, s, kind],
                ag_sems.at[1, l, s, kind],
                r,
                sibling,
            ).wait_recv()
        here = jnp.concatenate([normed[l, s, k] for k in range(cols)], axis=1)

        def rows_of(f):
            return jnp.dot(qkvg[l, f], here, preferred_element_type=jnp.float32)

        keys[s] = rows_of(1).astype(jnp.bfloat16)
        values[s] = rows_of(2).astype(jnp.bfloat16)
        query = rows_of(0)
        gating = jax.nn.sigmoid(rows_of(3))
        for k in range(cols):
            at = slice(k * tokens, (k + 1) * tokens)
            queries[s, k] = query[:, at].T.astype(jnp.bfloat16)
            gates[s, k] = gating[:, at]

    score_scale = 1.0 / math.sqrt(HEAD_DIM)

    def attend(l, block):
        live = jnp.concatenate([mask_buf[k][0:1] for k in range(rows)], axis=1) > 0
        square = lax.broadcasted_iota(jnp.int32, (tokens, tokens), 0) == lax.broadcasted_iota(
            jnp.int32, (tokens, tokens), 1
        )

        def one_sample(s, carry):
            for h in range(heads):
                at = slice(h * HEAD_DIM, (h + 1) * HEAD_DIM)
                scores = (
                    jnp.dot(
                        queries[s, block, :, at], keys[s, at], preferred_element_type=jnp.float32
                    )
                    * score_scale
                )
                head_bias = jnp.concatenate([spread[l, block, k, h] for k in range(cols)], axis=1)
                scores = scores + head_bias.astype(jnp.float32)
                scores = jnp.where(live, scores, MASKED)
                highest = jnp.max(scores, axis=-1, keepdims=True)
                exponent = jnp.exp(scores - highest)
                summed = jnp.sum(exponent, axis=-1, keepdims=True)
                mixed = lax.dot_general(
                    values[s, at],
                    exponent.astype(jnp.bfloat16),
                    NT,
                    preferred_element_type=jnp.float32,
                )
                summed_row = jnp.sum(jnp.where(square, summed, 0.0), axis=0, keepdims=True)
                attended = mixed * (1.0 / summed_row)
                gated_send[l, block, s, at] = (gates[s, block, at] * attended).astype(jnp.bfloat16)
            return carry

        lax.fori_loop(0, own, one_sample, 0)

        gap = lax.rem(block - c + cols, cols)

        @pl.when(block != c)
        def _():
            remote(
                gated_send.at[l, block],
                gated_recv.at[l, c],
                gated_sems.at[0, l, gap],
                gated_sems.at[1, l, gap],
                r,
                block,
            ).start()

        @pl.when(block == c)
        def _():
            gated_recv[l, c] = gated_send[l, block]

    def gated_wait(l):
        for d in range(1, cols):
            frm = col_of(cols - d)
            remote(
                gated_send.at[l, frm],
                gated_recv.at[l, frm],
                gated_sems.at[0, l, d],
                gated_sems.at[1, l, d],
                r,
                frm,
            ).wait_recv()

    for d in range(1, rows):
        frm = lax.rem(r + rows - d, rows)
        remote(
            mask, mask_buf.at[frm], mask_sems.at[0, d], mask_sems.at[1, d], frm, c
        ).wait_recv()

    for s in range(own):
        here = jnp.concatenate([stream_recv[f, s].astype(jnp.float32) for f in range(cols)], axis=0)
        stream[s] = here
        send_normed(0, s, here)

    for l in range(LAYERS):
        for s in range(own):
            forward_normed(l, s)
            if s == 0:
                advance(l, 0)
        if l + 1 < LAYERS:
            bias_exchange(l + 1)
        out_w_send(l)
        for s in range(own):
            project(l, s)

        def ring_round(t, carry, l=l):
            def side(k, inner):
                block = r - t + 2 * t * k

                @pl.when((block >= 0) & (block < rows) & (k <= t))
                def _():
                    attend(l, block)

                return inner

            lax.fori_loop(0, 2, side, 0)

            @pl.when((t >= 1) & (t < rows - 1))
            def _():
                advance(l, t)

            @pl.when(t == rows - 2)
            def _():
                if l + 1 < LAYERS:
                    bias_exchange_wait(l + 1)
                    ring_send(l + 1, 0)

            @pl.when(t == 1)
            def _():
                out_w_arrived(l, 1, across)
                remote(
                    out_full.at[across, l],
                    out_full.at[across, l],
                    out_w_sems.at[0, l, 2],
                    out_w_sems.at[1, l, 2],
                    r,
                    sibling,
                ).start()

            return carry

        lax.fori_loop(0, rows, ring_round, 0)
        out_w_arrived(l, 0, sibling)
        out_w_arrived(l, 2, far)
        gated_wait(l)
        joined = jnp.concatenate(
            [
                jnp.concatenate([gated_recv[l, k, s] for k in range(cols)], axis=0)
                for s in range(own)
            ],
            axis=1,
        )
        weight = jnp.concatenate([out_full[k, l] for k in range(cols)], axis=0)
        update = jnp.dot(weight, joined, preferred_element_type=jnp.float32)
        for s in range(own):
            here = stream[s] + update[:, s * tokens : (s + 1) * tokens]
            rounded = here.astype(jnp.bfloat16)
            here = rounded.astype(jnp.float32)
            if l + 1 < LAYERS:
                stream[s] = here
                send_normed(l + 1, s, here)
            else:
                for f in range(cols):
                    final_send[f, s] = here[f * width : (f + 1) * width].astype(jnp.bfloat16)

    place = pl.ds(r * own, own)

    def end_desc(f):
        return remote(final_send.at[f], out.at[place], end_sems.at[0, f], end_sems.at[1, r], c, f)

    for f in range(cols):
        stays = on_diag & (c == f)

        @pl.when(stays)
        def _(f=f):
            out[place] = final_send[f]

        @pl.when(jnp.logical_not(stays))
        def _(f=f):
            end_desc(f).start()

    for k in range(rows):

        @pl.when(jnp.logical_not(on_diag & (r == k)))
        def _(k=k):
            remote(
                final_send.at[0],
                out.at[pl.ds(k * own, own)],
                end_sems.at[0, 0],
                end_sems.at[1, k],
                k,
                r,
            ).wait_recv()

    for f in range(cols):

        @pl.when(jnp.logical_not(on_diag & (c == f)))
        def _(f=f):
            end_desc(f).wait_send()

    for desc in sent:
        desc.wait_send()

    @pl.when(jnp.logical_not(on_diag))
    def _():
        remote(
            stream_send.at[pl.ds(r * own, own)],
            stream_recv.at[c],
            in_sems.at[0, 0],
            in_sems.at[1, c],
            r,
            r,
        ).wait_send()

    for l in range(LAYERS):
        remote(
            out_full.at[across, l],
            out_full.at[across, l],
            out_w_sems.at[0, l, 2],
            out_w_sems.at[1, l, 2],
            r,
            sibling,
        ).wait_send()
        for step in range(rows - 1):
            ring_sent(l, step)
        for d in range(1, cols):
            to = col_of(d)
            remote(
                gated_send.at[l, to],
                gated_recv.at[l, c],
                gated_sems.at[0, l, d],
                gated_sems.at[1, l, d],
                r,
                to,
            ).wait_send()


def pair_bias(x_ref, w_ref, o_ref):
    lines, across, chans = x_ref.shape
    here = x_ref[...].reshape(lines * across, chans).astype(jnp.float32)
    rounded = layer_norm(here).astype(jnp.bfloat16)
    biases = lax.dot_general(w_ref[...], rounded, NT, preferred_element_type=jnp.float32)
    o_ref[...] = biases.reshape(w_ref.shape[0], lines, across).astype(jnp.bfloat16)


def per_device_fused(
    rows,
    cols,
    single,
    pair_act,
    token_mask,
    atom_feats,
    atom_token,
    atom_count,
    atom_weight,
    bias_weight,
    qkvg_weight,
    out_weight,
):
    samples, tokens, width = single.shape
    single = single.transpose(0, 2, 1)
    own = samples // rows
    depth = rows * tokens
    heads = width // HEAD_DIM
    full = width * cols
    chans = atom_feats.shape[1]
    slots = atom_feats.shape[0]
    lines, pairs = 16, pair_act.shape[2]
    all_heads = bias_weight.shape[1] * bias_weight.shape[2]
    biases = pl.pallas_call(
        pair_bias,
        grid=(tokens // lines,),
        in_specs=[
            pl.BlockSpec((lines, tokens, pairs), lambda i: (i, 0, 0)),
            pl.BlockSpec((all_heads, pairs), lambda i: (0, 0)),
        ],
        out_specs=pl.BlockSpec((all_heads, lines, tokens), lambda i: (0, i, 0)),
        out_shape=jax.ShapeDtypeStruct((all_heads, tokens, tokens), jnp.bfloat16),
        name="pair_bias",
    )(pair_act, bias_weight.reshape(pairs, all_heads).T)
    biases = biases.reshape(LAYERS, cols, heads, tokens, tokens)
    mask = jnp.broadcast_to((token_mask > 0).astype(jnp.float32)[None, :], (8, tokens))
    bf16, f32 = jnp.bfloat16, jnp.float32
    dma = pltpu.SemaphoreType.DMA
    updated = pl.pallas_call(
        lambda *refs: fused(rows, cols, *refs),
        out_shape=jax.ShapeDtypeStruct(single.shape, bf16),
        in_specs=[pl.BlockSpec(memory_space=pltpu.VMEM)] * 9,
        out_specs=pl.BlockSpec(memory_space=pltpu.VMEM),
        scratch_shapes=[
            pltpu.VMEM((LAYERS, rows, cols, heads, tokens, tokens), bf16),
            pltpu.VMEM((LAYERS, own, cols, full, tokens), bf16),
            pltpu.VMEM((cols, LAYERS, width, full), bf16),
            pltpu.VMEM((own, full, tokens), f32),
            pltpu.VMEM((cols, tokens + 16, chans), bf16),
            pltpu.VMEM((samples, width, tokens), bf16),
            pltpu.VMEM((cols, own, width, tokens), bf16),
            pltpu.VMEM((rows, 8, tokens), f32),
            pltpu.VMEM((own, rows, tokens, width), bf16),
            pltpu.VMEM((own, width, depth), bf16),
            pltpu.VMEM((own, width, depth), bf16),
            pltpu.VMEM((own, rows, width, tokens), f32),
            pltpu.VMEM((LAYERS, rows, own, width, tokens), bf16),
            pltpu.VMEM((LAYERS, cols, own, width, tokens), bf16),
            pltpu.VMEM((cols, own, width, tokens), bf16),
            dma((2, cols)),
            dma((2, rows)),
            dma((2, LAYERS, cols)),
            dma((2, LAYERS, 2, rows)),
            dma((2, LAYERS, 3)),
            dma((2, max(rows, cols))),
            dma((2, LAYERS, own, 3)),
            dma((2, LAYERS, cols)),
            dma((2, max(rows, cols))),
        ],
        compiler_params=pltpu.CompilerParams(
            collective_id=0, has_side_effects=True, vmem_limit_bytes=56 * 1024 * 1024
        ),
        name="fused_blocks",
    )(
        biases,
        single,
        atom_feats,
        atom_token.reshape(1, slots),
        atom_count.reshape(1, 1),
        atom_weight.T,
        mask,
        qkvg_weight,
        out_weight,
    )
    return updated.transpose(0, 2, 1)


def solution(mesh):
    rows, cols = mesh.shape["row"], mesh.shape["col"]
    placed = (
        P(None, ("parts", "row"), "col"),
        P(("parts", "row"), "col", None),
        P(("parts", "row")),
        P(("parts", "row", "col"), None),
        P(("parts", "row", "col")),
        P(("parts", "row", "col")),
        P(None, "col"),
        P(),
        P(None, None, "col", None),
        P(None, "col", None),
    )

    def body(single, *rest):
        pairs = rest[0].shape
        square = rows == cols == 4 and single.shape[0] % rows == 0 and pairs[0] == pairs[1]
        square = square and pairs[0] % 128 == 0
        if square and single.shape[2] % HEAD_DIM == 0:
            return per_device_fused(rows, cols, single, *rest)
        return per_device(single, *rest)

    return jax.shard_map(
        body,
        mesh=mesh,
        in_specs=placed,
        out_specs=P(None, ("parts", "row"), "col"),
        check_vma=False,
    )
```

profile of v0, /device:TPU:0, one launch (start us, length us, event | category | flops | bytes accessed | tf_op | source)
XLA Modules:
  0.0 127.4 jit_solution(8262137805577921971)
XLA Ops:
  0.7 0.7 compare_convert_fusion
  1.3 0.6 broadcast_in_dim.2.refs_6_
  1.9 9.1 %pair_bias.1 = bf16[32,128,128]{2,1,0:T(8,128)(2,1)} custom-call(bf16[128,128,128]{2,1,0:T(8,128)(2,1)} %x_ref.1, bf16[32,128]{1,0:T(8,128)(2,1)} %bitcast.14), custom_call_target="tpu_custom_call" | custom-call | tf_op jit(solution)/shard_map/pair_bias/pallas_call | solution.py:714
  11.1 114.5 %fused_blocks.1 = bf16[8,192,128]{2,1,0:T(8,128)(2,1)} custom-call(bf16[2,4,4,128,128]{4,3,2,1,0:T(8,128)(2,1)} %bitcast.10, bf16[8,192,128]{2,1,0:T(8,128)(2,1)} %bitcast.12, bf16[256,128]{1,0:T(8,128)(2,1)} %refs_2_.1, s32[1,256]{1,0:T(1,128)} %bitcast.15, s32[1,1]{1,0:T(1,128)} %bitcast.9.refs_4_, bf16[192,128]{1,0:T(8,128)(2,1)} %bitcast.13, ...), custom_call_target="tpu_custom_call" | custom-call | tf_op jit(solution)/shard_map/fused_blocks/pallas_call | solution.py:729
  125.6 1.8 %copy.13 = bf16[8,128,192]{1,2,0:T(8,128)(2,1)} copy(bf16[8,128,192]{1,2,0:T(8,128)(2,1)} %bitcast.11) | data formatting | bytes 786432
where the time goes:
time: 129 us; the launch traced here: 127 us
  Pallas kernels  124 us (96%)
  local copies, waits for them, and re-layouts  2.37 us (2%)
    pallas_call x1, Pallas kernels, per_device_fused(): pl.pallas_call(lambda *refs: fused(rows, cols, *refs), out_shape=jax.Shap...  115 us
    pallas_call x1, Pallas kernels, per_device_fused(): pl.pallas_call(pair_bias, grid=(tokens // lines,), in_specs=[pl.BlockSpec...  9.15 us

commit v1 on v0

v1 whole, which is shorter than its diff:
```python
import math

import jax
import jax.numpy as jnp
from jax import lax
from jax.experimental import pallas as pl
from jax.experimental.pallas import tpu as pltpu
from jax.sharding import PartitionSpec as P

HEAD_DIM = 48
LAYERS = 2


EPS = 1e-05
MASKED = -1000000000.0
START_LOW = -1e30


def layer_norm(values):
    average = jnp.mean(values, axis=-1, keepdims=True)
    centered = values - average
    variance = jnp.mean(centered * centered, axis=-1, keepdims=True)
    return centered * lax.rsqrt(variance + EPS)


def per_device(
    single,
    pair_act,
    token_mask,
    atom_feats,
    atom_token,
    atom_count,
    atom_weight,
    bias_weight,
    qkvg_weight,
    out_weight,
):
    tok_rows = single.shape[1]
    sample_count = single.shape[0]
    slot_ids = jnp.arange(atom_feats.shape[0], dtype=jnp.int32)
    live_slots = slot_ids < atom_count[0]
    token_ids = jnp.arange(tok_rows, dtype=jnp.int32)
    owner_match = (token_ids[:, None] == atom_token[None, :]) & live_slots[None, :]
    owners = owner_match.astype(jnp.float32)
    counts = jnp.sum(owners, axis=1)
    atom_sums = jnp.dot(
        owner_match.astype(jnp.bfloat16), atom_feats, preferred_element_type=jnp.float32
    )
    sum_total, count_total = (
        lax.psum(atom_sums.astype(jnp.bfloat16), "col").astype(jnp.float32),
        lax.psum(counts[:, None].astype(jnp.bfloat16), "col").astype(jnp.float32),
    )
    pooled = (
        jnp.dot(sum_total, atom_weight.astype(jnp.float32), precision=lax.Precision.HIGHEST)
        / count_total
    )
    stream = (single.astype(jnp.float32) + pooled[None]).astype(jnp.bfloat16)
    pair_normed = layer_norm(pair_act.astype(jnp.float32)).astype(jnp.bfloat16)
    biases = jnp.einsum(
        "ijc,clh->lhij", pair_normed, bias_weight, preferred_element_type=jnp.float32
    ).astype(jnp.bfloat16)
    live_keys = (token_mask > 0).astype(jnp.bfloat16)[None, :]
    score_scale = 1.0 / math.sqrt(HEAD_DIM)
    for layer_idx in range(LAYERS):
        spread = lax.all_to_all(biases[layer_idx], "col", split_axis=0, concat_axis=2, tiled=True)
        gathered = lax.all_gather(stream, "col", axis=2, tiled=True)
        normed = layer_norm(gathered.astype(jnp.float32)).astype(jnp.bfloat16)
        projected = jnp.einsum(
            "std,fed->fste", normed, qkvg_weight[layer_idx], preferred_element_type=jnp.float32
        )
        head_width = projected.shape[3]
        heads_here = head_width // HEAD_DIM
        queries = (
            projected[0].astype(jnp.bfloat16).reshape(sample_count, tok_rows, heads_here, HEAD_DIM)
        )
        key_rows = projected[1].astype(jnp.bfloat16)
        value_rows = projected[2].astype(jnp.bfloat16)
        gating = jax.nn.sigmoid(projected[3])

        def attend(running, incoming, offset, queries=queries, spread=spread):
            top_old, summed_old, acc_old = running
            keys_in, values_in, live_in = incoming
            key_count = keys_in.shape[1]
            keys_heads = keys_in.reshape(sample_count, key_count, heads_here, HEAD_DIM)
            values_heads = values_in.reshape(sample_count, key_count, heads_here, HEAD_DIM)
            scores = (
                jnp.einsum(
                    "sqhd,skhd->shqk", queries, keys_heads, preferred_element_type=jnp.float32
                )
                * score_scale
            )
            scores = scores + spread.astype(jnp.float32)[None]
            scores = jnp.where(live_in[0][None, None, None, :] > 0, scores, MASKED)
            top_new = jnp.maximum(top_old, jnp.max(scores, axis=-1))
            exponent = jnp.exp(scores - top_new[..., None])
            summed_new = jnp.sum(exponent, axis=-1)
            weights = exponent.astype(jnp.bfloat16)
            acc_new = jnp.einsum(
                "shqk,skhd->shqd", weights, values_heads, preferred_element_type=jnp.float32
            )
            return (top_new, summed_new, acc_new)

        start_state = (
            jnp.full((sample_count, heads_here, tok_rows), START_LOW, jnp.float32),
            jnp.zeros((sample_count, heads_here, tok_rows), jnp.float32),
            jnp.zeros((sample_count, heads_here, tok_rows, HEAD_DIM), jnp.float32),
        )
        top_end, summed_end, acc_end = attend(
            start_state,
            (
                lax.all_gather(key_rows, "row", axis=1, tiled=True),
                lax.all_gather(value_rows, "row", axis=1, tiled=True),
                lax.all_gather(live_keys, "row", axis=1, tiled=True),
            ),
            jnp.int32(0),
        )
        attended = acc_end / summed_end[..., None]
        attended = attended.transpose(0, 2, 1, 3).reshape(sample_count, tok_rows, head_width)
        gated = (gating * attended).astype(jnp.bfloat16)
        out_rows = out_weight[layer_idx]

        def project(summed, incoming, offset, out_rows=out_rows):
            return jnp.einsum("std,ed->ste", incoming, out_rows, preferred_element_type=jnp.float32)

        zero_update = jnp.zeros((sample_count, tok_rows, out_rows.shape[0]), jnp.float32)
        update = project(
            zero_update, lax.all_gather(gated, "col", axis=2, tiled=True), jnp.int32(0)
        )
        stream = (stream.astype(jnp.float32) + update).astype(jnp.bfloat16)
    return stream


MESH = pl.DeviceIdType.MESH
NT = (((1,), (1,)), ((), ()))


def remote(src, dst, send_sem, recv_sem, row, col):
    return pltpu.make_async_remote_copy(
        src_ref=src,
        dst_ref=dst,
        send_sem=send_sem,
        recv_sem=recv_sem,
        device_id={"row": row, "col": col},
        device_id_type=MESH,
    )


def fused(
    rows,
    cols,
    bias,
    single,
    feats,
    slot_token,
    slot_count,
    atom_weight,
    mask,
    qkvg,
    out_w,
    out,
    spread,
    stream,
    first,
    parts_buf,
    mask_buf,
    queries,
    keys,
    values,
    gates,
    gated,
    final,
    part_sems,
    mask_sems,
    a2a_sems,
    pair_sems,
    in_sems,
    ag_sems,
    swap_sems,
    gated_sems,
    end_sems,
):
    r = lax.axis_index("row")
    c = lax.axis_index("col")
    samples, width, tokens = single.shape
    group = samples // 2
    tasks = LAYERS * group
    full = width * cols
    heads = width // HEAD_DIM
    sibling = c + 1 - 2 * lax.rem(c, 2)
    across = lax.rem(c + 2, cols)
    far = lax.rem(sibling + 2, cols)
    side = lax.rem(r, 2)
    mine = lax.div(r, 2)
    other = 1 - mine
    near = r + 1 - 2 * side
    peer_rows = {1: near, 2: lax.rem(r + 2, rows), 3: lax.rem(near + 2, rows)}

    barrier = pltpu.get_barrier_semaphore()
    for dc in range(1, cols):
        pl.semaphore_signal(
            barrier,
            inc=1,
            device_id={"row": r, "col": lax.rem(c + dc, cols)},
            device_id_type=MESH,
        )
    for d in range(1, rows):
        pl.semaphore_signal(
            barrier, inc=1, device_id={"row": peer_rows[d], "col": c}, device_id_type=MESH
        )
    pl.semaphore_wait(barrier, cols - 1 + rows - 1)

    sent = []

    def begin(desc):
        desc.start()
        sent.append(desc)

    def col_of(d):
        return lax.rem(c + d, cols)

    def a2a_desc(l, d):
        to = col_of(d)
        return remote(
            bias.at[l, to],
            spread.at[l, side, c],
            a2a_sems.at[0, l, d],
            a2a_sems.at[1, l, d],
            r,
            to,
        )

    def a2a_arrived(l, d):
        frm = col_of(cols - d)
        remote(
            bias.at[l, frm],
            spread.at[l, side, frm],
            a2a_sems.at[0, l, d],
            a2a_sems.at[1, l, d],
            r,
            frm,
        ).wait_recv()

    def pair_desc(l, d):
        block = col_of(cols - d) if d else c
        src = spread.at[l, side, block] if d else bias.at[l, c]
        return remote(
            src,
            spread.at[l, side, block],
            pair_sems.at[0, l, d],
            pair_sems.at[1, l, d],
            near,
            c,
        )

    def pair_arrived(l, d):
        block = col_of(cols - d) if d else c
        remote(
            spread.at[l, 1 - side, block],
            spread.at[l, 1 - side, block],
            pair_sems.at[0, l, d],
            pair_sems.at[1, l, d],
            near,
            c,
        ).wait_recv()

    def bias_exchange(l):
        for d in (2, 3, 1):
            a2a_desc(l, d).start()
        pair_desc(l, 0).start()
        spread[l, side, c] = bias[l, c]

    def bias_pass(l):
        for d in (1, 2, 3):
            a2a_arrived(l, d)
            pair_desc(l, d).start()

    def bias_arrived(l):
        for d in range(cols):
            pair_arrived(l, d)

    for d in range(1, rows):
        begin(remote(mask, mask_buf.at[r], mask_sems.at[0, d], mask_sems.at[1, d], peer_rows[d], c))
    mask_buf[r] = mask[...]

    slots = feats.shape[0]
    token_ids = lax.broadcasted_iota(jnp.int32, (tokens, slots), 0)
    slot_ids = lax.broadcasted_iota(jnp.int32, (tokens, slots), 1)
    match = (token_ids == slot_token[...]) & (slot_ids < slot_count[...])
    owners = jnp.where(match, 1.0, 0.0).astype(jnp.bfloat16)
    parts_buf[c, 0:tokens] = jnp.dot(
        owners, feats[...], preferred_element_type=jnp.float32
    ).astype(jnp.bfloat16)
    parts_buf[c, tokens : tokens + 16] = lax.dot_general(
        jnp.ones((16, slots), jnp.bfloat16), owners, NT, preferred_element_type=jnp.float32
    ).astype(jnp.bfloat16)
    for d in range(1, cols):
        begin(
            remote(
                parts_buf.at[c],
                parts_buf.at[c],
                part_sems.at[0, d],
                part_sems.at[1, d],
                r,
                col_of(d),
            )
        )
    bias_exchange(0)
    for d in range(1, cols):
        frm = col_of(cols - d)
        remote(
            parts_buf.at[frm], parts_buf.at[frm], part_sems.at[0, d], part_sems.at[1, d], r, frm
        ).wait_recv()
    total = jnp.zeros((width, tokens), jnp.float32)
    count_row = jnp.zeros((1, tokens), jnp.float32)
    for k in range(cols):
        total = total + lax.dot_general(
            atom_weight[...], parts_buf[k, 0:tokens], NT, preferred_element_type=jnp.float32
        )
        count_row = count_row + parts_buf[k, tokens : tokens + 16].astype(jnp.float32)[0:1]
    pooled = total / count_row

    def in_desc(d, s):
        at = s + group * (side if d == 2 else 1 - side)
        return remote(
            first.at[at],
            stream.at[0, s, mine, c, side],
            in_sems.at[0, d, s],
            in_sems.at[1, d, s],
            peer_rows[d],
            c,
        )

    def in_arrived(d, s):
        half = mine if d == 1 else other
        block = side if d == 2 else 1 - side
        remote(
            first.at[s],
            stream.at[0, s, half, c, block],
            in_sems.at[0, d, s],
            in_sems.at[1, d, s],
            peer_rows[d],
            c,
        ).wait_recv()

    def start_sample(s):
        for k in range(2):
            at = s + group * k
            first[at] = (single[at].astype(jnp.float32) + pooled).astype(jnp.bfloat16)
        stream[0, s, mine, c, side] = first[s + group * side]
        for d in (1, 2, 3):
            begin(in_desc(d, s))

    def ag_desc(t, half, kind):
        l, s = lax.div(t, group), lax.rem(t, group)
        block = across if kind == 2 else c
        return remote(
            stream.at[l, s, half, block],
            stream.at[l, s, half, block],
            ag_sems.at[0, kind, t, half],
            ag_sems.at[1, kind, t, half],
            r,
            across if kind == 1 else sibling,
        )

    def ag_arrived(t, half, kind):
        l, s = lax.div(t, group), lax.rem(t, group)
        block = (sibling, across, far)[kind]
        remote(
            stream.at[l, s, half, block],
            stream.at[l, s, half, block],
            ag_sems.at[0, kind, t, half],
            ag_sems.at[1, kind, t, half],
            r,
            across if kind == 1 else sibling,
        ).wait_recv()

    def ag_send(t, half):
        ag_desc(t, half, 1).start()
        ag_desc(t, half, 0).start()

    def swap_desc(s):
        return remote(
            stream.at[1, s, mine, c],
            stream.at[1, s, mine, c],
            swap_sems.at[0, s],
            swap_sems.at[1, s],
            peer_rows[2],
            c,
        )

    def swap_arrived(s):
        remote(
            stream.at[1, s, other, c],
            stream.at[1, s, other, c],
            swap_sems.at[0, s],
            swap_sems.at[1, s],
            peer_rows[2],
            c,
        ).wait_recv()

    def stage(t):
        s = lax.rem(t, group)

        @pl.when(t < group)
        def _():
            in_arrived(1, s)
            ag_send(t, mine)
            in_arrived(2, s)
            in_arrived(3, s)
            ag_send(t, other)

        @pl.when(t >= group)
        def _():
            swap_arrived(s)
            ag_send(t, other)

    def forward(t):
        for half in (mine, other):
            ag_arrived(t, half, 1)
            ag_desc(t, half, 2).start()

    score_scale = 1.0 / math.sqrt(HEAD_DIM)

    def normed_half(l, s, half):
        here = jnp.concatenate(
            [
                jnp.concatenate([stream[l, s, half, k, b] for k in range(cols)], axis=0)
                for b in range(2)
            ],
            axis=1,
        ).astype(jnp.float32)
        average = jnp.mean(here, axis=0, keepdims=True)
        centered = here - average
        variance = jnp.mean(centered * centered, axis=0, keepdims=True)
        return (centered * lax.rsqrt(variance + EPS)).astype(jnp.bfloat16)

    def project(t):
        l, s = lax.div(t, group), lax.rem(t, group)
        for half in (mine, other):
            ag_arrived(t, half, 0)
            ag_arrived(t, half, 2)
            here = normed_half(l, s, half)

            def rows_of(f, here=here):
                return jnp.dot(qkvg[l, f], here, preferred_element_type=jnp.float32)

            keys[half] = rows_of(1).astype(jnp.bfloat16)
            values[half] = rows_of(2).astype(jnp.bfloat16)
            if half is mine:
                queries[...] = rows_of(0).T.astype(jnp.bfloat16)
                gates[...] = jax.nn.sigmoid(rows_of(3))

    def attend(t):
        l, s = lax.div(t, group), lax.rem(t, group)
        live = jnp.concatenate([mask_buf[k][0:1] for k in range(rows)], axis=1) > 0
        square = lax.broadcasted_iota(jnp.int32, (tokens, tokens), 0) == lax.broadcasted_iota(
            jnp.int32, (tokens, tokens), 1
        )
        for h in range(heads):
            at = slice(h * HEAD_DIM, (h + 1) * HEAD_DIM)
            key_here = jnp.concatenate([keys[k, at] for k in range(2)], axis=1)
            value_here = jnp.concatenate([values[k, at] for k in range(2)], axis=1)
            for b in range(2):
                cut = slice(b * tokens, (b + 1) * tokens)
                scores = (
                    jnp.dot(queries[cut, at], key_here, preferred_element_type=jnp.float32)
                    * score_scale
                )
                head_bias = jnp.concatenate([spread[l, b, k, h] for k in range(cols)], axis=1)
                scores = scores + head_bias.astype(jnp.float32)
                scores = jnp.where(live, scores, MASKED)
                highest = jnp.max(scores, axis=-1, keepdims=True)
                exponent = jnp.exp(scores - highest)
                summed = jnp.sum(exponent, axis=-1, keepdims=True)
                mixed = lax.dot_general(
                    value_here,
                    exponent.astype(jnp.bfloat16),
                    NT,
                    preferred_element_type=jnp.float32,
                )
                summed_row = jnp.sum(jnp.where(square, summed, 0.0), axis=0, keepdims=True)
                attended = mixed * (1.0 / summed_row)
                gated[l, s, c, at, cut] = (gates[at, cut] * attended).astype(jnp.bfloat16)

    def gated_desc(t, kind):
        l, s = lax.div(t, group), lax.rem(t, group)
        block = across if kind == 2 else c
        return remote(
            gated.at[l, s, block],
            gated.at[l, s, block],
            gated_sems.at[0, kind, t],
            gated_sems.at[1, kind, t],
            r,
            across if kind == 1 else sibling,
        )

    def gated_arrived(t, kind):
        l, s = lax.div(t, group), lax.rem(t, group)
        block = (sibling, across, far)[kind]
        remote(
            gated.at[l, s, block],
            gated.at[l, s, block],
            gated_sems.at[0, kind, t],
            gated_sems.at[1, kind, t],
            r,
            across if kind == 1 else sibling,
        ).wait_recv()

    def end_desc(s):
        return remote(
            final.at[s, 1 - side],
            out.at[side * group + s],
            end_sems.at[0, s],
            end_sems.at[1, s],
            near,
            c,
        )

    def finish(t):
        l, s = lax.div(t, group), lax.rem(t, group)
        gated_arrived(t, 1)
        gated_desc(t, 2).start()
        gated_arrived(t, 0)
        gated_arrived(t, 2)
        joined = jnp.concatenate([gated[l, s, k] for k in range(cols)], axis=0)
        update = jnp.dot(out_w[l], joined, preferred_element_type=jnp.float32)
        for b in range(2):
            cut = slice(b * tokens, (b + 1) * tokens)
            before = stream[l, s, mine, c, b].astype(jnp.float32)
            final[s, b] = (before + update[:, cut]).astype(jnp.bfloat16)

        @pl.when(l + 1 < LAYERS)
        def _():
            stream[1, s, mine, c] = final[s]
            swap_desc(s).start()
            ag_send(t + group, mine)

        @pl.when(l + 1 == LAYERS)
        def _():
            end_desc(s).start()
            out[side * group + s] = final[s, side]

    start_sample(0)
    start_sample(1)
    bias_pass(0)
    for s in range(2, group):
        start_sample(s)
    for d in range(1, rows):
        frm = peer_rows[d]
        remote(
            mask, mask_buf.at[frm], mask_sems.at[0, d], mask_sems.at[1, d], frm, c
        ).wait_recv()
    stage(jnp.int32(0))

    def step(t, carry):
        @pl.when(t + 1 < tasks)
        def _():
            stage(t + 1)

        @pl.when(t == 0)
        def _():
            bias_exchange(1)

        @pl.when(t < tasks)
        def _():
            forward(t)
            project(t)

        @pl.when(t == 0)
        def _():
            bias_arrived(0)

        @pl.when(t == group)
        def _():
            bias_arrived(1)

        @pl.when(t < tasks)
        def _():
            attend(t)
            gated_desc(t, 1).start()
            gated_desc(t, 0).start()

        @pl.when(t == 0)
        def _():
            bias_pass(1)

        @pl.when(t >= 1)
        def _():
            finish(t - 1)

        return carry

    lax.fori_loop(0, tasks + 1, step, 0)

    for s in range(group):
        place = (1 - side) * group + s
        remote(
            final.at[s, side], out.at[place], end_sems.at[0, s], end_sems.at[1, s], near, c
        ).wait_recv()

    for desc in sent:
        desc.wait_send()
    for l in range(LAYERS):
        for d in range(1, cols):
            a2a_desc(l, d).wait_send()
        for d in range(cols):
            pair_desc(l, d).wait_send()
    for s in range(group):
        swap_desc(s).wait_send()
        end_desc(s).wait_send()

    def drain(t, carry):
        for kind in range(3):
            for half in (mine, other):
                ag_desc(t, half, kind).wait_send()
            gated_desc(t, kind).wait_send()
        return carry

    lax.fori_loop(0, tasks, drain, 0)


def pair_bias(x_ref, w_ref, o_ref):
    lines, across, chans = x_ref.shape
    here = x_ref[...].reshape(lines * across, chans).astype(jnp.float32)
    rounded = layer_norm(here).astype(jnp.bfloat16)
    biases = lax.dot_general(w_ref[...], rounded, NT, preferred_element_type=jnp.float32)
    o_ref[...] = biases.reshape(w_ref.shape[0], lines, across).astype(jnp.bfloat16)


def per_device_fused(
    rows,
    cols,
    single,
    pair_act,
    token_mask,
    atom_feats,
    atom_token,
    atom_count,
    atom_weight,
    bias_weight,
    qkvg_weight,
    out_weight,
):
    samples, tokens, width = single.shape
    single = single.transpose(0, 2, 1)
    group = samples // 2
    heads = width // HEAD_DIM
    chans = atom_feats.shape[1]
    slots = atom_feats.shape[0]
    lines, pairs = 16, pair_act.shape[2]
    all_heads = bias_weight.shape[1] * bias_weight.shape[2]
    biases = pl.pallas_call(
        pair_bias,
        grid=(tokens // lines,),
        in_specs=[
            pl.BlockSpec((lines, tokens, pairs), lambda i: (i, 0, 0)),
            pl.BlockSpec((all_heads, pairs), lambda i: (0, 0)),
        ],
        out_specs=pl.BlockSpec((all_heads, lines, tokens), lambda i: (0, i, 0)),
        out_shape=jax.ShapeDtypeStruct((all_heads, tokens, tokens), jnp.bfloat16),
        name="pair_bias",
    )(pair_act, bias_weight.reshape(pairs, all_heads).T)
    biases = biases.reshape(LAYERS, cols, heads, tokens, tokens)
    mask = jnp.broadcast_to((token_mask > 0).astype(jnp.float32)[None, :], (8, tokens))
    bf16, f32 = jnp.bfloat16, jnp.float32
    dma = pltpu.SemaphoreType.DMA
    updated = pl.pallas_call(
        lambda *refs: fused(rows, cols, *refs),
        out_shape=jax.ShapeDtypeStruct(single.shape, bf16),
        in_specs=[pl.BlockSpec(memory_space=pltpu.VMEM)] * 9,
        out_specs=pl.BlockSpec(memory_space=pltpu.VMEM),
        scratch_shapes=[
            pltpu.VMEM((LAYERS, 2, cols, heads, tokens, tokens), bf16),
            pltpu.VMEM((LAYERS, group, 2, cols, 2, width, tokens), bf16),
            pltpu.VMEM((samples, width, tokens), bf16),
            pltpu.VMEM((cols, tokens + 16, chans), bf16),
            pltpu.VMEM((rows, 8, tokens), f32),
            pltpu.VMEM((2 * tokens, width), bf16),
            pltpu.VMEM((2, width, 2 * tokens), bf16),
            pltpu.VMEM((2, width, 2 * tokens), bf16),
            pltpu.VMEM((width, 2 * tokens), f32),
            pltpu.VMEM((LAYERS, group, cols, width, 2 * tokens), bf16),
            pltpu.VMEM((group, 2, width, tokens), bf16),
            dma((2, cols)),
            dma((2, rows)),
            dma((2, LAYERS, cols)),
            dma((2, LAYERS, cols)),
            dma((2, rows, group)),
            dma((2, 3, LAYERS * group, 2)),
            dma((2, group)),
            dma((2, 3, LAYERS * group)),
            dma((2, group)),
        ],
        compiler_params=pltpu.CompilerParams(
            collective_id=0, has_side_effects=True, vmem_limit_bytes=56 * 1024 * 1024
        ),
        name="fused_blocks",
    )(
        biases,
        single,
        atom_feats,
        atom_token.reshape(1, slots),
        atom_count.reshape(1, 1),
        atom_weight.T,
        mask,
        qkvg_weight,
        out_weight,
    )
    return updated.transpose(0, 2, 1)


def solution(mesh):
    rows, cols = mesh.shape["row"], mesh.shape["col"]
    placed = (
        P(None, ("parts", "row"), "col"),
        P(("parts", "row"), "col", None),
        P(("parts", "row")),
        P(("parts", "row", "col"), None),
        P(("parts", "row", "col")),
        P(("parts", "row", "col")),
        P(None, "col"),
        P(),
        P(None, None, "col", None),
        P(None, "col", None),
    )

    def body(single, *rest):
        pairs = rest[0].shape
        square = rows == cols == 4 and single.shape[0] % 4 == 0 and pairs[0] == pairs[1]
        square = square and pairs[0] % 128 == 0
        if square and single.shape[2] % HEAD_DIM == 0:
            return per_device_fused(rows, cols, single, *rest)
        return per_device(single, *rest)

    return jax.shard_map(
        body,
        mesh=mesh,
        in_specs=placed,
        out_specs=P(None, ("parts", "row"), "col"),
        check_vma=False,
    )
```

time: 129 us -> 99.9 us (0.77)
  Pallas kernels: 124 us -> 95.8 us
    pallas_call x1, Pallas kernels: 115 us -> 86.7 us  [per_device_fused(): pl.pallas_call(lambda *refs: fused(rows, cols, *refs), out_shape=jax.Shap...]
where the time goes in v1:
time: 99.9 us; the launch traced here: 99.5 us
  Pallas kernels  95.8 us (96%)
  local copies, waits for them, and re-layouts  2.37 us (2%)
    pallas_call x1, Pallas kernels, per_device_fused(): pl.pallas_call(lambda *refs: fused(rows, cols, *refs), out_shape=jax.Shap...  86.7 us
    pallas_call x1, Pallas kernels, per_device_fused(): pl.pallas_call(pair_bias, grid=(tokens // lines,), in_specs=[pl.BlockSpec...  9.15 us

profile of v1, /device:TPU:0, one launch (start us, length us, event | category | flops | bytes accessed | tf_op | source)
XLA Modules:
  0.0 99.5 jit_solution(8259159577889463941)
XLA Ops:
  0.7 0.7 compare_convert_fusion
  1.3 0.6 broadcast_in_dim.2.refs_6_
  1.9 9.1 %pair_bias.1 = bf16[32,128,128]{2,1,0:T(8,128)(2,1)} custom-call(bf16[128,128,128]{2,1,0:T(8,128)(2,1)} %x_ref.1, bf16[32,128]{1,0:T(8,128)(2,1)} %bitcast.14), custom_call_target="tpu_custom_call" | custom-call | tf_op jit(solution)/shard_map/pair_bias/pallas_call | solution.py:652
  11.1 86.7 %fused_blocks.1 = bf16[8,192,128]{2,1,0:T(8,128)(2,1)} custom-call(bf16[2,4,4,128,128]{4,3,2,1,0:T(8,128)(2,1)} %bitcast.10, bf16[8,192,128]{2,1,0:T(8,128)(2,1)} %bitcast.12, bf16[256,128]{1,0:T(8,128)(2,1)} %refs_2_.1, s32[1,256]{1,0:T(1,128)} %bitcast.15, s32[1,1]{1,0:T(1,128)} %bitcast.9.refs_4_, bf16[192,128]{1,0:T(8,128)(2,1)} %bitcast.13, ...), custom_call_target="tpu_custom_call" | custom-call | tf_op jit(solution)/shard_map/fused_blocks/pallas_call | solution.py:667
  97.8 1.8 %copy.13 = bf16[8,128,192]{1,2,0:T(8,128)(2,1)} copy(bf16[8,128,192]{1,2,0:T(8,128)(2,1)} %bitcast.11) | data formatting | bytes 786432

commit v2 on v1

--- a/solution.py
+++ b/solution.py
@@ -9,6 +9,7 @@
 
 HEAD_DIM = 48
 LAYERS = 2
+CHUNKS = 4
 
 
 EPS = 1e-05
@@ -148,16 +149,21 @@
 def fused(
     rows,
     cols,
-    bias,
+    pair_hbm,
+    bias_w,
     single,
     feats,
     slot_token,
     slot_count,
     atom_weight,
     mask,
+    qkvg_hbm,
+    out_w_hbm,
+    out,
+    pair,
+    bias,
     qkvg,
     out_w,
-    out,
     spread,
     stream,
     first,
@@ -178,6 +184,7 @@
     swap_sems,
     gated_sems,
     end_sems,
+    load_sems,
 ):
     r = lax.axis_index("row")
     c = lax.axis_index("col")
@@ -195,6 +202,18 @@
     near = r + 1 - 2 * side
     peer_rows = {1: near, 2: lax.rem(r + 2, rows), 3: lax.rem(near + 2, rows)}
 
+    lines = tokens // CHUNKS
+
+    def load(k):
+        if k < CHUNKS:
+            at = pl.ds(k * lines, lines)
+            return pltpu.make_async_copy(pair_hbm.at[at], pair.at[at], load_sems.at[k])
+        src, dst = ((qkvg_hbm, qkvg), (out_w_hbm, out_w))[k - CHUNKS]
+        return pltpu.make_async_copy(src, dst, load_sems.at[k])
+
+    for k in range(CHUNKS + 2):
+        load(k).start()
+
     barrier = pltpu.get_barrier_semaphore()
     for dc in range(1, cols):
         pl.semaphore_signal(
@@ -207,8 +226,6 @@
         pl.semaphore_signal(
             barrier, inc=1, device_id={"row": peer_rows[d], "col": c}, device_id_type=MESH
         )
-    pl.semaphore_wait(barrier, cols - 1 + rows - 1)
-
     sent = []
 
     def begin(desc):
@@ -218,69 +235,70 @@
     def col_of(d):
         return lax.rem(c + d, cols)
 
-    def a2a_desc(l, d):
+    def rows_at(k):
+        return pl.ds(k * lines, lines)
+
+    def bias_chunk(k):
+        load(k).wait()
+        here = pair_normed(pair[rows_at(k)].reshape(lines * tokens, pair.shape[2]))
+        made = lax.dot_general(bias_w[...], here, NT, preferred_element_type=jnp.float32)
+        made = made.astype(jnp.bfloat16).reshape(LAYERS, cols, heads, lines, tokens)
+        bias[:, :, :, rows_at(k)] = made
+
+    def a2a_desc(l, d, k):
         to = col_of(d)
         return remote(
-            bias.at[l, to],
-            spread.at[l, side, c],
-            a2a_sems.at[0, l, d],
-            a2a_sems.at[1, l, d],
+            bias.at[l, to, :, rows_at(k)],
+            spread.at[l, side, c, :, rows_at(k)],
+            a2a_sems.at[0, l, d, k],
+            a2a_sems.at[1, l, d, k],
             r,
             to,
         )
 
-    def a2a_arrived(l, d):
+    def a2a_arrived(l, d, k):
         frm = col_of(cols - d)
         remote(
-            bias.at[l, frm],
-            spread.at[l, side, frm],
-            a2a_sems.at[0, l, d],
-            a2a_sems.at[1, l, d],
+            bias.at[l, frm, :, rows_at(k)],
+            spread.at[l, side, frm, :, rows_at(k)],
+            a2a_sems.at[0, l, d, k],
+            a2a_sems.at[1, l, d, k],
             r,
             frm,
         ).wait_recv()
 
-    def pair_desc(l, d):
+    def pair_desc(l, d, k):
         block = col_of(cols - d) if d else c
-        src = spread.at[l, side, block] if d else bias.at[l, c]
+        held = spread.at[l, side, block, :, rows_at(k)]
         return remote(
-            src,
-            spread.at[l, side, block],
-            pair_sems.at[0, l, d],
-            pair_sems.at[1, l, d],
+            held if d else bias.at[l, c, :, rows_at(k)],
+            held,
+            pair_sems.at[0, l, d, k],
+            pair_sems.at[1, l, d, k],
             near,
             c,
         )
 
-    def pair_arrived(l, d):
+    def pair_arrived(l, d, k):
         block = col_of(cols - d) if d else c
-        remote(
-            spread.at[l, 1 - side, block],
-            spread.at[l, 1 - side, block],
-            pair_sems.at[0, l, d],
-            pair_sems.at[1, l, d],
-            near,
-            c,
-        ).wait_recv()
-
-    def bias_exchange(l):
+        held = spread.at[l, 1 - side, block, :, rows_at(k)]
+        remote(held, held, pair_sems.at[0, l, d, k], pair_sems.at[1, l, d, k], near, c).wait_recv()
+
+    def bias_exchange(l, k):
         for d in (2, 3, 1):
-            a2a_desc(l, d).start()
-        pair_desc(l, 0).start()
-        spread[l, side, c] = bias[l, c]
-
-    def bias_pass(l):
+            a2a_desc(l, d, k).start()
+        pair_desc(l, 0, k).start()
+        spread[l, side, c, :, rows_at(k)] = bias[l, c, :, rows_at(k)]
+
+    def bias_pass(l, k):
         for d in (1, 2, 3):
-            a2a_arrived(l, d)
-            pair_desc(l, d).start()
+            a2a_arrived(l, d, k)
+            pair_desc(l, d, k).start()
 
     def bias_arrived(l):
-        for d in range(cols):
-            pair_arrived(l, d)
-
-    for d in range(1, rows):
-        begin(remote(mask, mask_buf.at[r], mask_sems.at[0, d], mask_sems.at[1, d], peer_rows[d], c))
-    mask_buf[r] = mask[...]
+        for k in range(CHUNKS):
+            for d in range(cols):
+                pair_arrived(l, d, k)
 
     slots = feats.shape[0]
     token_ids = lax.broadcasted_iota(jnp.int32, (tokens, slots), 0)
@@ -293,6 +311,8 @@
     parts_buf[c, tokens : tokens + 16] = lax.dot_general(
         jnp.ones((16, slots), jnp.bfloat16), owners, NT, preferred_element_type=jnp.float32
     ).astype(jnp.bfloat16)
+    bias_chunk(0)
+    pl.semaphore_wait(barrier, cols - 1 + rows - 1)
     for d in range(1, cols):
         begin(
             remote(
@@ -304,7 +324,13 @@
                 col_of(d),
             )
         )
-    bias_exchange(0)
+    for d in range(1, rows):
+        begin(remote(mask, mask_buf.at[r], mask_sems.at[0, d], mask_sems.at[1, d], peer_rows[d], c))
+    mask_buf[r] = mask[...]
+
+    bias_exchange(0, 0)
+    bias_chunk(1)
+    bias_exchange(0, 1)
     for d in range(1, cols):
         frm = col_of(cols - d)
         remote(
@@ -452,7 +478,7 @@
 
     def attend(t):
         l, s = lax.div(t, group), lax.rem(t, group)
-        live = jnp.concatenate([mask_buf[k][0:1] for k in range(rows)], axis=1) > 0
+        live = jnp.concatenate([mask_buf[k] for k in range(rows)], axis=1) > 0
         square = lax.broadcasted_iota(jnp.int32, (tokens, tokens), 0) == lax.broadcasted_iota(
             jnp.int32, (tokens, tokens), 1
         )
@@ -541,25 +567,29 @@
             out[side * group + s] = final[s, side]
 
     start_sample(0)
-    start_sample(1)
-    bias_pass(0)
-    for s in range(2, group):
+    for k in range(2, CHUNKS):
+        bias_chunk(k)
+        bias_exchange(0, k)
+        bias_pass(0, k - 2)
+    stage(jnp.int32(0))
+    for k in range(CHUNKS - 2, CHUNKS):
+        bias_pass(0, k)
+    for s in range(1, group):
         start_sample(s)
+    for k in range(CHUNKS):
+        bias_exchange(1, k)
     for d in range(1, rows):
         frm = peer_rows[d]
         remote(
             mask, mask_buf.at[frm], mask_sems.at[0, d], mask_sems.at[1, d], frm, c
         ).wait_recv()
-    stage(jnp.int32(0))
+    load(CHUNKS).wait()
+    load(CHUNKS + 1).wait()
 
     def step(t, carry):
         @pl.when(t + 1 < tasks)
         def _():
             stage(t + 1)
-
-        @pl.when(t == 0)
-        def _():
-            bias_exchange(1)
 
         @pl.when(t < tasks)
         def _():
@@ -582,7 +612,8 @@
 
         @pl.when(t == 0)
         def _():
-            bias_pass(1)
+            for k in range(CHUNKS):
+                bias_pass(1, k)
 
         @pl.when(t >= 1)
         def _():
@@ -601,10 +632,11 @@
     for desc in sent:
         desc.wait_send()
     for l in range(LAYERS):
-        for d in range(1, cols):
-            a2a_desc(l, d).wait_send()
-        for d in range(cols):
-            pair_desc(l, d).wait_send()
+        for k in range(CHUNKS):
+            for d in range(1, cols):
+                a2a_desc(l, d, k).wait_send()
+            for d in range(cols):
+                pair_desc(l, d, k).wait_send()
     for s in range(group):
         swap_desc(s).wait_send()
         end_desc(s).wait_send()
@@ -619,12 +651,22 @@
     lax.fori_loop(0, tasks, drain, 0)
 
 
-def pair_bias(x_ref, w_ref, o_ref):
-    lines, across, chans = x_ref.shape
-    here = x_ref[...].reshape(lines * across, chans).astype(jnp.float32)
-    rounded = layer_norm(here).astype(jnp.bfloat16)
-    biases = lax.dot_general(w_ref[...], rounded, NT, preferred_element_type=jnp.float32)
-    o_ref[...] = biases.reshape(w_ref.shape[0], lines, across).astype(jnp.bfloat16)
+def pair_normed(rows_in):
+    chans = rows_in.shape[1]
+    if chans & (chans - 1):
+        return layer_norm(rows_in.astype(jnp.float32)).astype(jnp.bfloat16)
+    share = jnp.full((chans, chans), 1.0 / chans, jnp.bfloat16)
+    average = jnp.dot(rows_in, share, preferred_element_type=jnp.float32)
+    centered = rows_in.astype(jnp.float32) - average
+    square = centered * centered
+    high = square.astype(jnp.bfloat16)
+    low = (square - high.astype(jnp.float32)).astype(jnp.bfloat16)
+    variance = jnp.dot(
+        jnp.concatenate([high, low], axis=1),
+        jnp.concatenate([share, share], axis=0),
+        preferred_element_type=jnp.float32,
+    )
+    return (centered * lax.rsqrt(variance + EPS)).astype(jnp.bfloat16)
 
 
 def per_device_fused(
@@ -647,34 +689,27 @@
     heads = width // HEAD_DIM
     chans = atom_feats.shape[1]
     slots = atom_feats.shape[0]
-    lines, pairs = 16, pair_act.shape[2]
+    pairs = pair_act.shape[2]
     all_heads = bias_weight.shape[1] * bias_weight.shape[2]
-    biases = pl.pallas_call(
-        pair_bias,
-        grid=(tokens // lines,),
-        in_specs=[
-            pl.BlockSpec((lines, tokens, pairs), lambda i: (i, 0, 0)),
-            pl.BlockSpec((all_heads, pairs), lambda i: (0, 0)),
-        ],
-        out_specs=pl.BlockSpec((all_heads, lines, tokens), lambda i: (0, i, 0)),
-        out_shape=jax.ShapeDtypeStruct((all_heads, tokens, tokens), jnp.bfloat16),
-        name="pair_bias",
-    )(pair_act, bias_weight.reshape(pairs, all_heads).T)
-    biases = biases.reshape(LAYERS, cols, heads, tokens, tokens)
-    mask = jnp.broadcast_to((token_mask > 0).astype(jnp.float32)[None, :], (8, tokens))
     bf16, f32 = jnp.bfloat16, jnp.float32
     dma = pltpu.SemaphoreType.DMA
     updated = pl.pallas_call(
         lambda *refs: fused(rows, cols, *refs),
         out_shape=jax.ShapeDtypeStruct(single.shape, bf16),
-        in_specs=[pl.BlockSpec(memory_space=pltpu.VMEM)] * 9,
+        in_specs=[pl.BlockSpec(memory_space=pl.ANY)]
+        + [pl.BlockSpec(memory_space=pltpu.VMEM)] * 7
+        + [pl.BlockSpec(memory_space=pl.ANY)] * 2,
         out_specs=pl.BlockSpec(memory_space=pltpu.VMEM),
         scratch_shapes=[
+            pltpu.VMEM(pair_act.shape, bf16),
+            pltpu.VMEM((LAYERS, cols, heads, tokens, tokens), bf16),
+            pltpu.VMEM(qkvg_weight.shape, bf16),
+            pltpu.VMEM(out_weight.shape, bf16),
             pltpu.VMEM((LAYERS, 2, cols, heads, tokens, tokens), bf16),
             pltpu.VMEM((LAYERS, group, 2, cols, 2, width, tokens), bf16),
             pltpu.VMEM((samples, width, tokens), bf16),
             pltpu.VMEM((cols, tokens + 16, chans), bf16),
-            pltpu.VMEM((rows, 8, tokens), f32),
+            pltpu.VMEM((rows, 1, tokens), jnp.int32),
             pltpu.VMEM((2 * tokens, width), bf16),
             pltpu.VMEM((2, width, 2 * tokens), bf16),
             pltpu.VMEM((2, width, 2 * tokens), bf16),
@@ -683,26 +718,28 @@
             pltpu.VMEM((group, 2, width, tokens), bf16),
             dma((2, cols)),
             dma((2, rows)),
-            dma((2, LAYERS, cols)),
-            dma((2, LAYERS, cols)),
+            dma((2, LAYERS, cols, CHUNKS)),
+            dma((2, LAYERS, cols, CHUNKS)),
             dma((2, rows, group)),
             dma((2, 3, LAYERS * group, 2)),
             dma((2, group)),
             dma((2, 3, LAYERS * group)),
             dma((2, group)),
+            dma((CHUNKS + 2,)),
         ],
         compiler_params=pltpu.CompilerParams(
             collective_id=0, has_side_effects=True, vmem_limit_bytes=56 * 1024 * 1024
         ),
         name="fused_blocks",
     )(
-        biases,
+        pair_act,
+        bias_weight.reshape(pairs, all_heads).T,
         single,
         atom_feats,
         atom_token.reshape(1, slots),
         atom_count.reshape(1, 1),
         atom_weight.T,
-        mask,
+        token_mask.reshape(1, tokens),
         qkvg_weight,
         out_weight,
     )

time: 99.9 us -> 93 us (0.931)
  Pallas kernels: 95.8 us -> 90.4 us
    pallas_call x1 -> x0, Pallas kernels: 9.15 us -> none  [per_device_fused(): pl.pallas_call(pair_bias, grid=(tokens // lines,), in_specs=[pl.BlockSpec...]
    pallas_call x1, Pallas kernels: 86.7 us -> 90.4 us  [per_device_fused(): pl.pallas_call(lambda *refs: fused(rows, cols, *refs), out_shape=jax.Shap...]
where the time goes in v2:
time: 93 us; the launch traced here: 92.8 us
  Pallas kernels  90.4 us (97%)
  local copies, waits for them, and re-layouts  1.77 us (2%)
    pallas_call x1, Pallas kernels, per_device_fused(): pl.pallas_call(lambda *refs: fused(rows, cols, *refs), out_shape=jax.Shap...  90.4 us

profile of v2, /device:TPU:0, one launch (start us, length us, event | category | flops | bytes accessed | tf_op | source)
XLA Modules:
  0.0 92.8 jit_solution(5651065656046579311)
XLA Ops:
  0.7 90.4 %fused_blocks.1 = bf16[8,192,128]{2,1,0:T(8,128)(2,1)} custom-call(bf16[128,128,128]{2,1,0:T(8,128)(2,1)} %refs_0_.1, bf16[32,128]{1,0:T(8,128)(2,1)} %bitcast.13, bf16[8,192,128]{2,1,0:T(8,128)(2,1)} %bitcast.11, bf16[256,128]{1,0:T(8,128)(2,1)} %refs_3_.1, s32[1,256]{1,0:T(1,128)} %bitcast.14, s32[1,1]{1,0:T(1,128)} %bitcast.9.refs_5_, ...), custom_call_target="tpu_custom_call" | custom-call | tf_op jit(solution)/shard_map/fused_blocks/pallas_call | solution.py:696
  91.1 1.8 %copy.13 = bf16[8,128,192]{1,2,0:T(8,128)(2,1)} copy(bf16[8,128,192]{1,2,0:T(8,128)(2,1)} %bitcast.10) | data formatting | bytes 786432

commit v3 on v2

--- a/solution.py
+++ b/solution.py
@@ -10,6 +10,7 @@
 HEAD_DIM = 48
 LAYERS = 2
 CHUNKS = 4
+RELAYED = 0
 
 
 EPS = 1e-05
@@ -168,6 +169,7 @@
     stream,
     first,
     parts_buf,
+    pooled,
     mask_buf,
     queries,
     keys,
@@ -195,7 +197,6 @@
     heads = width // HEAD_DIM
     sibling = c + 1 - 2 * lax.rem(c, 2)
     across = lax.rem(c + 2, cols)
-    far = lax.rem(sibling + 2, cols)
     side = lax.rem(r, 2)
     mine = lax.div(r, 2)
     other = 1 - mine
@@ -226,12 +227,6 @@
         pl.semaphore_signal(
             barrier, inc=1, device_id={"row": peer_rows[d], "col": c}, device_id_type=MESH
         )
-    sent = []
-
-    def begin(desc):
-        desc.start()
-        sent.append(desc)
-
     def col_of(d):
         return lax.rem(c + d, cols)
 
@@ -245,27 +240,19 @@
         made = made.astype(jnp.bfloat16).reshape(LAYERS, cols, heads, lines, tokens)
         bias[:, :, :, rows_at(k)] = made
 
+    def settle(ref, sem):
+        pltpu.make_async_copy(ref, ref, sem).wait()
+
     def a2a_desc(l, d, k):
         to = col_of(d)
         return remote(
             bias.at[l, to, :, rows_at(k)],
             spread.at[l, side, c, :, rows_at(k)],
-            a2a_sems.at[0, l, d, k],
-            a2a_sems.at[1, l, d, k],
+            a2a_sems.at[l, CHUNKS],
+            a2a_sems.at[l, k],
             r,
             to,
         )
-
-    def a2a_arrived(l, d, k):
-        frm = col_of(cols - d)
-        remote(
-            bias.at[l, frm, :, rows_at(k)],
-            spread.at[l, side, frm, :, rows_at(k)],
-            a2a_sems.at[0, l, d, k],
-            a2a_sems.at[1, l, d, k],
-            r,
-            frm,
-        ).wait_recv()
 
     def pair_desc(l, d, k):
         block = col_of(cols - d) if d else c
@@ -273,32 +260,28 @@
         return remote(
             held if d else bias.at[l, c, :, rows_at(k)],
             held,
-            pair_sems.at[0, l, d, k],
-            pair_sems.at[1, l, d, k],
+            pair_sems.at[0, l],
+            pair_sems.at[1, l],
             near,
             c,
         )
-
-    def pair_arrived(l, d, k):
-        block = col_of(cols - d) if d else c
-        held = spread.at[l, 1 - side, block, :, rows_at(k)]
-        remote(held, held, pair_sems.at[0, l, d, k], pair_sems.at[1, l, d, k], near, c).wait_recv()
 
     def bias_exchange(l, k):
         for d in (2, 3, 1):
             a2a_desc(l, d, k).start()
-        pair_desc(l, 0, k).start()
+        if l == 0:
+            pair_desc(l, 0, k).start()
         spread[l, side, c, :, rows_at(k)] = bias[l, c, :, rows_at(k)]
 
     def bias_pass(l, k):
-        for d in (1, 2, 3):
-            a2a_arrived(l, d, k)
+        if l:
+            pair_desc(l, 0, k).start()
+        settle(spread.at[l, side, pl.ds(0, cols - 1), :, rows_at(k)], a2a_sems.at[l, k])
+        for d in range(1, cols):
             pair_desc(l, d, k).start()
 
     def bias_arrived(l):
-        for k in range(CHUNKS):
-            for d in range(cols):
-                pair_arrived(l, d, k)
+        settle(spread.at[l, 1 - side], pair_sems.at[1, l])
 
     slots = feats.shape[0]
     token_ids = lax.broadcasted_iota(jnp.int32, (tokens, slots), 0)
@@ -314,28 +297,17 @@
     bias_chunk(0)
     pl.semaphore_wait(barrier, cols - 1 + rows - 1)
     for d in range(1, cols):
-        begin(
-            remote(
-                parts_buf.at[c],
-                parts_buf.at[c],
-                part_sems.at[0, d],
-                part_sems.at[1, d],
-                r,
-                col_of(d),
-            )
-        )
+        remote(
+            parts_buf.at[c], parts_buf.at[c], part_sems.at[0], part_sems.at[1], r, col_of(d)
+        ).start()
     for d in range(1, rows):
-        begin(remote(mask, mask_buf.at[r], mask_sems.at[0, d], mask_sems.at[1, d], peer_rows[d], c))
+        remote(mask, mask_buf.at[r], mask_sems.at[0], mask_sems.at[1], peer_rows[d], c).start()
     mask_buf[r] = mask[...]
 
     bias_exchange(0, 0)
     bias_chunk(1)
     bias_exchange(0, 1)
-    for d in range(1, cols):
-        frm = col_of(cols - d)
-        remote(
-            parts_buf.at[frm], parts_buf.at[frm], part_sems.at[0, d], part_sems.at[1, d], r, frm
-        ).wait_recv()
+    settle(parts_buf.at[pl.ds(0, cols - 1)], part_sems.at[1])
     total = jnp.zeros((width, tokens), jnp.float32)
     count_row = jnp.zeros((1, tokens), jnp.float32)
     for k in range(cols):
@@ -343,38 +315,26 @@
             atom_weight[...], parts_buf[k, 0:tokens], NT, preferred_element_type=jnp.float32
         )
         count_row = count_row + parts_buf[k, tokens : tokens + 16].astype(jnp.float32)[0:1]
-    pooled = total / count_row
+    pooled[...] = total / count_row
 
     def in_desc(d, s):
         at = s + group * (side if d == 2 else 1 - side)
         return remote(
             first.at[at],
             stream.at[0, s, mine, c, side],
-            in_sems.at[0, d, s],
-            in_sems.at[1, d, s],
+            in_sems.at[2, 0],
+            in_sems.at[min(d, 2) - 1, s],
             peer_rows[d],
             c,
         )
-
-    def in_arrived(d, s):
-        half = mine if d == 1 else other
-        block = side if d == 2 else 1 - side
-        remote(
-            first.at[s],
-            stream.at[0, s, half, c, block],
-            in_sems.at[0, d, s],
-            in_sems.at[1, d, s],
-            peer_rows[d],
-            c,
-        ).wait_recv()
 
     def start_sample(s):
         for k in range(2):
             at = s + group * k
-            first[at] = (single[at].astype(jnp.float32) + pooled).astype(jnp.bfloat16)
+            first[at] = (single[at].astype(jnp.float32) + pooled[...]).astype(jnp.bfloat16)
         stream[0, s, mine, c, side] = first[s + group * side]
         for d in (1, 2, 3):
-            begin(in_desc(d, s))
+            in_desc(d, s).start()
 
     def ag_desc(t, half, kind):
         l, s = lax.div(t, group), lax.rem(t, group)
@@ -382,23 +342,16 @@
         return remote(
             stream.at[l, s, half, block],
             stream.at[l, s, half, block],
-            ag_sems.at[0, kind, t, half],
-            ag_sems.at[1, kind, t, half],
+            ag_sems.at[t, 4],
+            ag_sems.at[t, 2 * half + kind % 2],
             r,
             across if kind == 1 else sibling,
         )
 
     def ag_arrived(t, half, kind):
         l, s = lax.div(t, group), lax.rem(t, group)
-        block = (sibling, across, far)[kind]
-        remote(
-            stream.at[l, s, half, block],
-            stream.at[l, s, half, block],
-            ag_sems.at[0, kind, t, half],
-            ag_sems.at[1, kind, t, half],
-            r,
-            across if kind == 1 else sibling,
-        ).wait_recv()
+        held = stream.at[l, s, half, across] if kind else stream.at[l, s, half, pl.ds(0, 2)]
+        settle(held, ag_sems.at[t, 2 * half + kind])
 
     def ag_send(t, half):
         ag_desc(t, half, 1).start()
@@ -408,42 +361,38 @@
         return remote(
             stream.at[1, s, mine, c],
             stream.at[1, s, mine, c],
-            swap_sems.at[0, s],
-            swap_sems.at[1, s],
+            swap_sems.at[group],
+            swap_sems.at[s],
             peer_rows[2],
             c,
         )
 
-    def swap_arrived(s):
-        remote(
-            stream.at[1, s, other, c],
-            stream.at[1, s, other, c],
-            swap_sems.at[0, s],
-            swap_sems.at[1, s],
-            peer_rows[2],
-            c,
-        ).wait_recv()
-
-    def stage(t):
+    def relay_desc(t):
+        held = stream.at[1, lax.rem(t, group), mine, across]
+        return remote(
+            held, held, ag_sems.at[t, 4], ag_sems.at[t, 2 * mine + 1], peer_rows[2], c
+        )
+
+    def stage_first(t, half):
+        if half is mine:
+            settle(first.at[0], in_sems.at[0, t])
+        else:
+            settle(stream.at[0, t, other, c], in_sems.at[1, t])
+        ag_send(t, half)
+
+    def stage_next(t):
         s = lax.rem(t, group)
-
-        @pl.when(t < group)
-        def _():
-            in_arrived(1, s)
-            ag_send(t, mine)
-            in_arrived(2, s)
-            in_arrived(3, s)
-            ag_send(t, other)
-
-        @pl.when(t >= group)
-        def _():
-            swap_arrived(s)
-            ag_send(t, other)
-
-    def forward(t):
-        for half in (mine, other):
-            ag_arrived(t, half, 1)
-            ag_desc(t, half, 2).start()
+        settle(stream.at[1, s, other, c], swap_sems.at[s])
+
+        @pl.when(t < tasks - RELAYED)
+        def _():
+            ag_desc(t, other, 1).start()
+
+        ag_desc(t, other, 0).start()
+
+    def forward(t, half):
+        ag_arrived(t, half, 1)
+        ag_desc(t, half, 2).start()
 
     score_scale = 1.0 / math.sqrt(HEAD_DIM)
 
@@ -464,7 +413,6 @@
         l, s = lax.div(t, group), lax.rem(t, group)
         for half in (mine, other):
             ag_arrived(t, half, 0)
-            ag_arrived(t, half, 2)
             here = normed_half(l, s, half)
 
             def rows_of(f, here=here):
@@ -514,40 +462,30 @@
         return remote(
             gated.at[l, s, block],
             gated.at[l, s, block],
-            gated_sems.at[0, kind, t],
-            gated_sems.at[1, kind, t],
+            gated_sems.at[2, 0],
+            gated_sems.at[kind % 2, t],
             r,
             across if kind == 1 else sibling,
         )
-
-    def gated_arrived(t, kind):
-        l, s = lax.div(t, group), lax.rem(t, group)
-        block = (sibling, across, far)[kind]
-        remote(
-            gated.at[l, s, block],
-            gated.at[l, s, block],
-            gated_sems.at[0, kind, t],
-            gated_sems.at[1, kind, t],
-            r,
-            across if kind == 1 else sibling,
-        ).wait_recv()
 
     def end_desc(s):
         return remote(
             final.at[s, 1 - side],
             out.at[side * group + s],
-            end_sems.at[0, s],
-            end_sems.at[1, s],
+            end_sems.at[0],
+            end_sems.at[1],
             near,
             c,
         )
 
+    def pass_gated(t):
+        l, s = lax.div(t, group), lax.rem(t, group)
+        settle(gated.at[l, s, across], gated_sems.at[1, t])
+        gated_desc(t, 2).start()
+
     def finish(t):
         l, s = lax.div(t, group), lax.rem(t, group)
-        gated_arrived(t, 1)
-        gated_desc(t, 2).start()
-        gated_arrived(t, 0)
-        gated_arrived(t, 2)
+        settle(gated.at[l, s, pl.ds(0, 2)], gated_sems.at[0, t])
         joined = jnp.concatenate([gated[l, s, k] for k in range(cols)], axis=0)
         update = jnp.dot(out_w[l], joined, preferred_element_type=jnp.float32)
         for b in range(2):
@@ -571,30 +509,33 @@
         bias_chunk(k)
         bias_exchange(0, k)
         bias_pass(0, k - 2)
-    stage(jnp.int32(0))
-    for k in range(CHUNKS - 2, CHUNKS):
-        bias_pass(0, k)
-    for s in range(1, group):
-        start_sample(s)
+    stage_first(0, mine)
+    bias_pass(0, CHUNKS - 2)
+    start_sample(1)
+    bias_pass(0, CHUNKS - 1)
+    stage_first(0, other)
     for k in range(CHUNKS):
         bias_exchange(1, k)
-    for d in range(1, rows):
-        frm = peer_rows[d]
-        remote(
-            mask, mask_buf.at[frm], mask_sems.at[0, d], mask_sems.at[1, d], frm, c
-        ).wait_recv()
+    settle(mask_buf.at[pl.ds(0, rows - 1)], mask_sems.at[1])
     load(CHUNKS).wait()
     load(CHUNKS + 1).wait()
 
+    forward(0, mine)
+    forward(0, other)
+
     def step(t, carry):
-        @pl.when(t + 1 < tasks)
-        def _():
-            stage(t + 1)
-
         @pl.when(t < tasks)
         def _():
-            forward(t)
             project(t)
+
+        @pl.when(t + 1 < group)
+        def _():
+            stage_first(t + 1, mine)
+            stage_first(t + 1, other)
+
+        @pl.when(t + 2 < group)
+        def _():
+            start_sample(t + 2)
 
         @pl.when(t == 0)
         def _():
@@ -610,42 +551,60 @@
             gated_desc(t, 1).start()
             gated_desc(t, 0).start()
 
-        @pl.when(t == 0)
-        def _():
-            for k in range(CHUNKS):
+        for k in range(CHUNKS):
+
+            @pl.when(t == max(k - 1, 0))
+            def _(k=k):
                 bias_pass(1, k)
 
-        @pl.when(t >= 1)
+        @pl.when((t >= 1) & (t < tasks))
+        def _():
+            pass_gated(t - 1)
+
+        @pl.when(t + 1 < tasks - RELAYED)
+        def _():
+            forward(t + 1, mine)
+
+        @pl.when((t + 2 >= tasks - RELAYED) & (t + 2 < tasks))
+        def _():
+            forward(t + 2, mine)
+            relay_desc(t + 2).start()
+
+        @pl.when((t >= 1) & (t <= group))
         def _():
             finish(t - 1)
 
+        @pl.when(t >= group + 2)
+        def _():
+            finish(t - 2)
+
+        @pl.when(t + 1 < tasks)
+        def _():
+            forward(t + 1, other)
+
+        @pl.when((t + 2 >= group) & (t + 2 < tasks))
+        def _():
+            stage_next(t + 2)
+
         return carry
 
     lax.fori_loop(0, tasks + 1, step, 0)
-
-    for s in range(group):
-        place = (1 - side) * group + s
-        remote(
-            final.at[s, side], out.at[place], end_sems.at[0, s], end_sems.at[1, s], near, c
-        ).wait_recv()
-
-    for desc in sent:
-        desc.wait_send()
+    pass_gated(tasks - 1)
+    finish(jnp.int32(tasks - 1))
+
+    settle(out.at[pl.ds((1 - side) * group, group)], end_sems.at[1])
+    settle(parts_buf.at[pl.ds(0, cols - 1)], part_sems.at[0])
+    settle(mask_buf.at[pl.ds(0, rows - 1)], mask_sems.at[0])
     for l in range(LAYERS):
-        for k in range(CHUNKS):
-            for d in range(1, cols):
-                a2a_desc(l, d, k).wait_send()
-            for d in range(cols):
-                pair_desc(l, d, k).wait_send()
-    for s in range(group):
-        swap_desc(s).wait_send()
-        end_desc(s).wait_send()
+        settle(spread.at[l, 0, pl.ds(0, cols - 1)], a2a_sems.at[l, CHUNKS])
+        settle(spread.at[l, 0], pair_sems.at[0, l])
+    settle(stream.at[0, pl.ds(0, group), 0, pl.ds(0, 3), 0], in_sems.at[2, 0])
+    settle(stream.at[1, pl.ds(0, group), 0, 0], swap_sems.at[group])
+    settle(gated.at[:, :, pl.ds(0, 3)], gated_sems.at[2, 0])
+    settle(out.at[pl.ds(0, group)], end_sems.at[0])
 
     def drain(t, carry):
-        for kind in range(3):
-            for half in (mine, other):
-                ag_desc(t, half, kind).wait_send()
-            gated_desc(t, kind).wait_send()
+        settle(stream.at[0, 0, :, pl.ds(0, 3)], ag_sems.at[t, 4])
         return carry
 
     lax.fori_loop(0, tasks, drain, 0)
@@ -709,6 +668,7 @@
             pltpu.VMEM((LAYERS, group, 2, cols, 2, width, tokens), bf16),
             pltpu.VMEM((samples, width, tokens), bf16),
             pltpu.VMEM((cols, tokens + 16, chans), bf16),
+            pltpu.VMEM((width, tokens), f32),
             pltpu.VMEM((rows, 1, tokens), jnp.int32),
             pltpu.VMEM((2 * tokens, width), bf16),
             pltpu.VMEM((2, width, 2 * tokens), bf16),
@@ -716,15 +676,15 @@
             pltpu.VMEM((width, 2 * tokens), f32),
             pltpu.VMEM((LAYERS, group, cols, width, 2 * tokens), bf16),
             pltpu.VMEM((group, 2, width, tokens), bf16),
-            dma((2, cols)),
-            dma((2, rows)),
-            dma((2, LAYERS, cols, CHUNKS)),
-            dma((2, LAYERS, cols, CHUNKS)),
-            dma((2, rows, group)),
-            dma((2, 3, LAYERS * group, 2)),
-            dma((2, group)),
-            dma((2, 3, LAYERS * group)),
-            dma((2, group)),
+            dma((2,)),
+            dma((2,)),
+            dma((LAYERS, CHUNKS + 1)),
+            dma((2, LAYERS)),
+            dma((3, group)),
+            dma((LAYERS * group, 5)),
+            dma((group + 1,)),
+            dma((3, LAYERS * group)),
+            dma((2,)),
             dma((CHUNKS + 2,)),
         ],
         compiler_params=pltpu.CompilerParams(

time: 93 us -> 86.9 us (0.934)
  Pallas kernels: 90.4 us -> 84.2 us
    pallas_call x1, Pallas kernels: 90.4 us -> 84.2 us  [per_device_fused(): pl.pallas_call(lambda *refs: fused(rows, cols, *refs), out_shape=jax.Shap...]
where the time goes in v3:
time: 86.9 us; the launch traced here: 86.6 us
  Pallas kernels  84.2 us (97%)
  local copies, waits for them, and re-layouts  1.77 us (2%)
    pallas_call x1, Pallas kernels, per_device_fused(): pl.pallas_call(lambda *refs: fused(rows, cols, *refs), out_shape=jax.Shap...  84.2 us
    unnamed x1, local copies, waits for them, and re-layouts  1.77 us

profile of v3, /device:TPU:0, one launch (start us, length us, event | category | flops | bytes accessed | tf_op | source)
XLA Modules:
  0.0 86.6 jit_solution(16141312532018075532)
XLA Ops:
  0.7 84.2 %fused_blocks.1 = bf16[8,192,128]{2,1,0:T(8,128)(2,1)} custom-call(bf16[128,128,128]{2,1,0:T(8,128)(2,1)} %refs_0_.1, bf16[32,128]{1,0:T(8,128)(2,1)} %bitcast.13, bf16[8,192,128]{2,1,0:T(8,128)(2,1)} %bitcast.11, bf16[256,128]{1,0:T(8,128)(2,1)} %refs_3_.1, s32[1,256]{1,0:T(1,128)} %bitcast.14, s32[1,1]{1,0:T(1,128)} %bitcast.9.refs_5_, ...), custom_call_target="tpu_custom_call" | custom-call | tf_op jit(solution)/shard_map/fused_blocks/pallas_call | solution.py:655
  84.8 1.8 %copy.13 = bf16[8,128,192]{1,2,0:T(8,128)(2,1)} copy(bf16[8,128,192]{1,2,0:T(8,128)(2,1)} %bitcast.10) | data formatting | bytes 786432

commit v4 on v3

--- a/solution.py
+++ b/solution.py
@@ -10,7 +10,6 @@
 HEAD_DIM = 48
 LAYERS = 2
 CHUNKS = 4
-RELAYED = 0
 
 
 EPS = 1e-05
@@ -151,6 +150,17 @@
     rows,
     cols,
     pair_hbm,
+    bias_w_hbm,
+    single_hbm,
+    feats_hbm,
+    slot_token_hbm,
+    slot_count_hbm,
+    atom_weight_hbm,
+    mask_hbm,
+    qkvg_hbm,
+    out_w_hbm,
+    out,
+    pair,
     bias_w,
     single,
     feats,
@@ -158,13 +168,9 @@
     slot_count,
     atom_weight,
     mask,
-    qkvg_hbm,
-    out_w_hbm,
-    out,
-    pair,
-    bias,
     qkvg,
     out_w,
+    bias,
     spread,
     stream,
     first,
@@ -205,14 +211,26 @@
 
     lines = tokens // CHUNKS
 
+    small = (
+        (feats_hbm, feats),
+        (slot_token_hbm, slot_token),
+        (slot_count_hbm, slot_count),
+        (bias_w_hbm, bias_w),
+        (mask_hbm, mask),
+        (atom_weight_hbm, atom_weight),
+        (single_hbm, single),
+        (qkvg_hbm, qkvg),
+        (out_w_hbm, out_w),
+    )
+
     def load(k):
         if k < CHUNKS:
             at = pl.ds(k * lines, lines)
             return pltpu.make_async_copy(pair_hbm.at[at], pair.at[at], load_sems.at[k])
-        src, dst = ((qkvg_hbm, qkvg), (out_w_hbm, out_w))[k - CHUNKS]
+        src, dst = small[k - CHUNKS]
         return pltpu.make_async_copy(src, dst, load_sems.at[k])
 
-    for k in range(CHUNKS + 2):
+    for k in (0, *range(CHUNKS, CHUNKS + 5), *range(1, CHUNKS), *range(CHUNKS + 5, CHUNKS + 9)):
         load(k).start()
 
     barrier = pltpu.get_barrier_semaphore()
@@ -284,6 +302,8 @@
         settle(spread.at[l, 1 - side], pair_sems.at[1, l])
 
     slots = feats.shape[0]
+    for k in range(5):
+        load(CHUNKS + k).wait()
     token_ids = lax.broadcasted_iota(jnp.int32, (tokens, slots), 0)
     slot_ids = lax.broadcasted_iota(jnp.int32, (tokens, slots), 1)
     match = (token_ids == slot_token[...]) & (slot_ids < slot_count[...])
@@ -308,6 +328,8 @@
     bias_chunk(1)
     bias_exchange(0, 1)
     settle(parts_buf.at[pl.ds(0, cols - 1)], part_sems.at[1])
+    load(CHUNKS + 5).wait()
+    load(CHUNKS + 6).wait()
     total = jnp.zeros((width, tokens), jnp.float32)
     count_row = jnp.zeros((1, tokens), jnp.float32)
     for k in range(cols):
@@ -367,12 +389,6 @@
             c,
         )
 
-    def relay_desc(t):
-        held = stream.at[1, lax.rem(t, group), mine, across]
-        return remote(
-            held, held, ag_sems.at[t, 4], ag_sems.at[t, 2 * mine + 1], peer_rows[2], c
-        )
-
     def stage_first(t, half):
         if half is mine:
             settle(first.at[0], in_sems.at[0, t])
@@ -383,12 +399,7 @@
     def stage_next(t):
         s = lax.rem(t, group)
         settle(stream.at[1, s, other, c], swap_sems.at[s])
-
-        @pl.when(t < tasks - RELAYED)
-        def _():
-            ag_desc(t, other, 1).start()
-
-        ag_desc(t, other, 0).start()
+        ag_send(t, other)
 
     def forward(t, half):
         ag_arrived(t, half, 1)
@@ -421,49 +432,64 @@
             keys[half] = rows_of(1).astype(jnp.bfloat16)
             values[half] = rows_of(2).astype(jnp.bfloat16)
             if half is mine:
-                queries[...] = rows_of(0).T.astype(jnp.bfloat16)
-                gates[...] = jax.nn.sigmoid(rows_of(3))
-
-    def attend(t):
+                query, gating = rows_of(0).T.astype(jnp.bfloat16), jax.nn.sigmoid(rows_of(3))
+                for b in range(2):
+                    queries[b] = query[b * tokens : (b + 1) * tokens]
+                    gates[b] = gating[:, b * tokens : (b + 1) * tokens]
+
+    def attend(t, last=False):
         l, s = lax.div(t, group), lax.rem(t, group)
         live = jnp.concatenate([mask_buf[k] for k in range(rows)], axis=1) > 0
         square = lax.broadcasted_iota(jnp.int32, (tokens, tokens), 0) == lax.broadcasted_iota(
             jnp.int32, (tokens, tokens), 1
         )
-        for h in range(heads):
+
+        def one(h, b):
             at = slice(h * HEAD_DIM, (h + 1) * HEAD_DIM)
             key_here = jnp.concatenate([keys[k, at] for k in range(2)], axis=1)
             value_here = jnp.concatenate([values[k, at] for k in range(2)], axis=1)
-            for b in range(2):
-                cut = slice(b * tokens, (b + 1) * tokens)
-                scores = (
-                    jnp.dot(queries[cut, at], key_here, preferred_element_type=jnp.float32)
-                    * score_scale
-                )
-                head_bias = jnp.concatenate([spread[l, b, k, h] for k in range(cols)], axis=1)
-                scores = scores + head_bias.astype(jnp.float32)
-                scores = jnp.where(live, scores, MASKED)
-                highest = jnp.max(scores, axis=-1, keepdims=True)
-                exponent = jnp.exp(scores - highest)
-                summed = jnp.sum(exponent, axis=-1, keepdims=True)
-                mixed = lax.dot_general(
-                    value_here,
-                    exponent.astype(jnp.bfloat16),
-                    NT,
-                    preferred_element_type=jnp.float32,
-                )
-                summed_row = jnp.sum(jnp.where(square, summed, 0.0), axis=0, keepdims=True)
-                attended = mixed * (1.0 / summed_row)
-                gated[l, s, c, at, cut] = (gates[at, cut] * attended).astype(jnp.bfloat16)
-
-    def gated_desc(t, kind):
+            scores = (
+                jnp.dot(queries[b, :, at], key_here, preferred_element_type=jnp.float32)
+                * score_scale
+            )
+            head_bias = jnp.concatenate([spread[l, b, k, h] for k in range(cols)], axis=1)
+            scores = scores + head_bias.astype(jnp.float32)
+            scores = jnp.where(live, scores, MASKED)
+            highest = jnp.max(scores, axis=-1, keepdims=True)
+            exponent = jnp.exp(scores - highest)
+            summed = jnp.sum(exponent, axis=-1, keepdims=True)
+            mixed = lax.dot_general(
+                value_here,
+                exponent.astype(jnp.bfloat16),
+                NT,
+                preferred_element_type=jnp.float32,
+            )
+            summed_row = jnp.sum(jnp.where(square, summed, 0.0), axis=0, keepdims=True)
+            attended = mixed * (1.0 / summed_row)
+            gated[l, s, b, c, at] = (gates[b, at] * attended).astype(jnp.bfloat16)
+
+        if last:
+            for b in (1 - side, side):
+                for h in range(heads):
+                    one(h, b)
+                gated_desc(t, 1, b).start()
+                gated_desc(t, 0, b).start()
+        else:
+            for h in range(heads):
+                for b in range(2):
+                    one(h, b)
+            gated_desc(t, 1).start()
+            gated_desc(t, 0).start()
+
+    def gated_desc(t, kind, b=None):
         l, s = lax.div(t, group), lax.rem(t, group)
         block = across if kind == 2 else c
+        held = gated.at[l, s, :, block] if b is None else gated.at[l, s, b, block]
         return remote(
-            gated.at[l, s, block],
-            gated.at[l, s, block],
-            gated_sems.at[2, 0],
-            gated_sems.at[kind % 2, t],
+            held,
+            held,
+            gated_sems.at[2, 0, 0],
+            gated_sems.at[kind % 2, 0 if b is None else b, t],
             r,
             across if kind == 1 else sibling,
         )
@@ -480,13 +506,31 @@
 
     def pass_gated(t):
         l, s = lax.div(t, group), lax.rem(t, group)
-        settle(gated.at[l, s, across], gated_sems.at[1, t])
+        settle(gated.at[l, s, :, across], gated_sems.at[1, 0, t])
         gated_desc(t, 2).start()
+
+    def pass_last(t, b):
+        l, s = LAYERS - 1, lax.rem(t, group)
+        settle(gated.at[l, s, b, across], gated_sems.at[1, b, t])
+        gated_desc(t, 2, b).start()
+
+    def finish_last(t, b):
+        l, s = LAYERS - 1, lax.rem(t, group)
+        settle(gated.at[l, s, b, pl.ds(0, 2)], gated_sems.at[0, b, t])
+        joined = jnp.concatenate([gated[l, s, b, k] for k in range(cols)], axis=0)
+        update = jnp.dot(out_w[l], joined, preferred_element_type=jnp.float32)
+        return (stream[l, s, mine, c, b].astype(jnp.float32) + update).astype(jnp.bfloat16)
 
     def finish(t):
         l, s = lax.div(t, group), lax.rem(t, group)
-        settle(gated.at[l, s, pl.ds(0, 2)], gated_sems.at[0, t])
-        joined = jnp.concatenate([gated[l, s, k] for k in range(cols)], axis=0)
+        settle(gated.at[l, s, :, pl.ds(0, 2)], gated_sems.at[0, 0, t])
+        joined = jnp.concatenate(
+            [
+                jnp.concatenate([gated[l, s, b, k] for k in range(cols)], axis=0)
+                for b in range(2)
+            ],
+            axis=1,
+        )
         update = jnp.dot(out_w[l], joined, preferred_element_type=jnp.float32)
         for b in range(2):
             cut = slice(b * tokens, (b + 1) * tokens)
@@ -509,66 +553,58 @@
         bias_chunk(k)
         bias_exchange(0, k)
         bias_pass(0, k - 2)
+        if k == 2:
+            start_sample(1)
     stage_first(0, mine)
     bias_pass(0, CHUNKS - 2)
-    start_sample(1)
+    stage_first(0, other)
     bias_pass(0, CHUNKS - 1)
-    stage_first(0, other)
+    start_sample(2)
+    stage_first(1, mine)
+    forward(0, mine)
+    stage_first(1, other)
     for k in range(CHUNKS):
         bias_exchange(1, k)
     settle(mask_buf.at[pl.ds(0, rows - 1)], mask_sems.at[1])
-    load(CHUNKS).wait()
-    load(CHUNKS + 1).wait()
-
-    forward(0, mine)
+    load(CHUNKS + 7).wait()
+    load(CHUNKS + 8).wait()
+
     forward(0, other)
 
     def step(t, carry):
-        @pl.when(t < tasks)
-        def _():
-            project(t)
-
-        @pl.when(t + 1 < group)
-        def _():
-            stage_first(t + 1, mine)
-            stage_first(t + 1, other)
-
-        @pl.when(t + 2 < group)
-        def _():
-            start_sample(t + 2)
-
-        @pl.when(t == 0)
-        def _():
-            bias_arrived(0)
-
-        @pl.when(t == group)
-        def _():
-            bias_arrived(1)
-
-        @pl.when(t < tasks)
-        def _():
-            attend(t)
-            gated_desc(t, 1).start()
-            gated_desc(t, 0).start()
+        project(t)
 
         for k in range(CHUNKS):
 
-            @pl.when(t == max(k - 1, 0))
+            @pl.when(t == max(k, 1))
             def _(k=k):
                 bias_pass(1, k)
 
-        @pl.when((t >= 1) & (t < tasks))
+        @pl.when(t == 0)
+        def _():
+            bias_arrived(0)
+
+        @pl.when(t == group)
+        def _():
+            bias_arrived(1)
+
+        @pl.when(t == 0)
+        def _():
+            for s in range(3, group):
+                start_sample(s)
+
+        attend(t)
+
+        @pl.when(t >= 1)
         def _():
             pass_gated(t - 1)
 
-        @pl.when(t + 1 < tasks - RELAYED)
-        def _():
-            forward(t + 1, mine)
-
-        @pl.when((t + 2 >= tasks - RELAYED) & (t + 2 < tasks))
-        def _():
-            forward(t + 2, mine)
-            relay_desc(t + 2).start()
+        @pl.when(t + 2 < group)
+        def _():
+            stage_first(t + 2, mine)
+            stage_first(t + 2, other)
+
+        forward(t + 1, mine)
 
         @pl.when((t >= 1) & (t <= group))
         def _():
@@ -578,19 +614,26 @@
         def _():
             finish(t - 2)
 
-        @pl.when(t + 1 < tasks)
-        def _():
-            forward(t + 1, other)
-
         @pl.when((t + 2 >= group) & (t + 2 < tasks))
         def _():
             stage_next(t + 2)
 
+        forward(t + 1, other)
+
         return carry
 
-    lax.fori_loop(0, tasks + 1, step, 0)
-    pass_gated(tasks - 1)
-    finish(jnp.int32(tasks - 1))
+    lax.fori_loop(0, tasks - 1, step, 0)
+    final_task = jnp.int32(tasks - 1)
+    project(final_task)
+    attend(final_task, True)
+    pass_gated(final_task - 1)
+    for k in (2, 1):
+        finish(final_task - k)
+    for b in (1 - side, side):
+        pass_last(final_task, b)
+    final[group - 1, 1 - side] = finish_last(final_task, 1 - side)
+    end_desc(group - 1).start()
+    out[side * group + group - 1] = finish_last(final_task, side)
 
     settle(out.at[pl.ds((1 - side) * group, group)], end_sems.at[1])
     settle(parts_buf.at[pl.ds(0, cols - 1)], part_sems.at[0])
@@ -600,7 +643,7 @@
         settle(spread.at[l, 0], pair_sems.at[0, l])
     settle(stream.at[0, pl.ds(0, group), 0, pl.ds(0, 3), 0], in_sems.at[2, 0])
     settle(stream.at[1, pl.ds(0, group), 0, 0], swap_sems.at[group])
-    settle(gated.at[:, :, pl.ds(0, 3)], gated_sems.at[2, 0])
+    settle(gated.at[:, :, :, pl.ds(0, 3)], gated_sems.at[2, 0, 0])
     settle(out.at[pl.ds(0, group)], end_sems.at[0])
 
     def drain(t, carry):
@@ -618,13 +661,7 @@
     average = jnp.dot(rows_in, share, preferred_element_type=jnp.float32)
     centered = rows_in.astype(jnp.float32) - average
     square = centered * centered
-    high = square.astype(jnp.bfloat16)
-    low = (square - high.astype(jnp.float32)).astype(jnp.bfloat16)
-    variance = jnp.dot(
-        jnp.concatenate([high, low], axis=1),
-        jnp.concatenate([share, share], axis=0),
-        preferred_element_type=jnp.float32,
-    )
+    variance = jnp.dot(square.astype(jnp.bfloat16), share, preferred_element_type=jnp.float32)
     return (centered * lax.rsqrt(variance + EPS)).astype(jnp.bfloat16)
 
 
@@ -655,26 +692,31 @@
     updated = pl.pallas_call(
         lambda *refs: fused(rows, cols, *refs),
         out_shape=jax.ShapeDtypeStruct(single.shape, bf16),
-        in_specs=[pl.BlockSpec(memory_space=pl.ANY)]
-        + [pl.BlockSpec(memory_space=pltpu.VMEM)] * 7
-        + [pl.BlockSpec(memory_space=pl.ANY)] * 2,
+        in_specs=[pl.BlockSpec(memory_space=pl.ANY)] * 10,
         out_specs=pl.BlockSpec(memory_space=pltpu.VMEM),
         scratch_shapes=[
             pltpu.VMEM(pair_act.shape, bf16),
-            pltpu.VMEM((LAYERS, cols, heads, tokens, tokens), bf16),
+            pltpu.VMEM((all_heads, pairs), bf16),
+            pltpu.VMEM(single.shape, bf16),
+            pltpu.VMEM(atom_feats.shape, bf16),
+            pltpu.VMEM((1, slots), jnp.int32),
+            pltpu.VMEM((1, 1), jnp.int32),
+            pltpu.VMEM((width, chans), bf16),
+            pltpu.VMEM((1, tokens), jnp.int32),
             pltpu.VMEM(qkvg_weight.shape, bf16),
             pltpu.VMEM(out_weight.shape, bf16),
+            pltpu.VMEM((LAYERS, cols, heads, tokens, tokens), bf16),
             pltpu.VMEM((LAYERS, 2, cols, heads, tokens, tokens), bf16),
             pltpu.VMEM((LAYERS, group, 2, cols, 2, width, tokens), bf16),
             pltpu.VMEM((samples, width, tokens), bf16),
             pltpu.VMEM((cols, tokens + 16, chans), bf16),
             pltpu.VMEM((width, tokens), f32),
             pltpu.VMEM((rows, 1, tokens), jnp.int32),
-            pltpu.VMEM((2 * tokens, width), bf16),
+            pltpu.VMEM((2, tokens, width), bf16),
             pltpu.VMEM((2, width, 2 * tokens), bf16),
             pltpu.VMEM((2, width, 2 * tokens), bf16),
-            pltpu.VMEM((width, 2 * tokens), f32),
-            pltpu.VMEM((LAYERS, group, cols, width, 2 * tokens), bf16),
+            pltpu.VMEM((2, width, tokens), f32),
+            pltpu.VMEM((LAYERS, group, 2, cols, width, tokens), bf16),
             pltpu.VMEM((group, 2, width, tokens), bf16),
             dma((2,)),
             dma((2,)),
@@ -683,9 +725,9 @@
             dma((3, group)),
             dma((LAYERS * group, 5)),
             dma((group + 1,)),
-            dma((3, LAYERS * group)),
+            dma((3, 2, LAYERS * group)),
             dma((2,)),
-            dma((CHUNKS + 2,)),
+            dma((CHUNKS + 9,)),
         ],
         compiler_params=pltpu.CompilerParams(
             collective_id=0, has_side_effects=True, vmem_limit_bytes=56 * 1024 * 1024

time: 86.9 us -> 84.6 us (0.974)
  Pallas kernels: 84.2 us -> 82 us
    pallas_call x1, Pallas kernels: 84.2 us -> 82 us  [per_device_fused(): pl.pallas_call(lambda *refs: fused(rows, cols, *refs), out_shape=jax.Shap...]
where the time goes in v4:
time: 84.6 us; the launch traced here: 84.4 us
  Pallas kernels  82 us (97%)
  local copies, waits for them, and re-layouts  1.77 us (2%)
    pallas_call x1, Pallas kernels, per_device_fused(): pl.pallas_call(lambda *refs: fused(rows, cols, *refs), out_shape=jax.Shap...  82 us
    unnamed x1, local copies, waits for them, and re-layouts  1.77 us

profile of v4, /device:TPU:0, one launch (start us, length us, event | category | flops | bytes accessed | tf_op | source)
XLA Modules:
  0.0 84.4 jit_solution(7775261023341061928)
XLA Ops:
  0.7 82.0 %fused_blocks.1 = bf16[8,192,128]{2,1,0:T(8,128)(2,1)} custom-call(bf16[128,128,128]{2,1,0:T(8,128)(2,1)} %refs_0_.1, bf16[32,128]{1,0:T(8,128)(2,1)} %bitcast.13, bf16[8,192,128]{2,1,0:T(8,128)(2,1)} %bitcast.11, bf16[256,128]{1,0:T(8,128)(2,1)} %refs_3_.1, s32[1,256]{1,0:T(1,128)} %bitcast.14, s32[1,1]{1,0:T(1,128)} %bitcast.9.refs_5_, ...), custom_call_target="tpu_custom_call" | custom-call | tf_op jit(solution)/shard_map/fused_blocks/pallas_call | solution.py:692
  82.7 1.8 %copy.13 = bf16[8,128,192]{1,2,0:T(8,128)(2,1)} copy(bf16[8,128,192]{1,2,0:T(8,128)(2,1)} %bitcast.10) | data formatting | bytes 786432

commit v5 on v4

--- a/solution.py
+++ b/solution.py
@@ -325,8 +325,9 @@
     mask_buf[r] = mask[...]
 
     bias_exchange(0, 0)
-    bias_chunk(1)
-    bias_exchange(0, 1)
+    for k in range(1, CHUNKS):
+        bias_chunk(k)
+        bias_exchange(0, k)
     settle(parts_buf.at[pl.ds(0, cols - 1)], part_sems.at[1])
     load(CHUNKS + 5).wait()
     load(CHUNKS + 6).wait()
@@ -421,7 +422,7 @@
         return (centered * lax.rsqrt(variance + EPS)).astype(jnp.bfloat16)
 
     def project(t):
-        l, s = lax.div(t, group), lax.rem(t, group)
+        l, s, slot = lax.div(t, group), lax.rem(t, group), lax.rem(t, 2)
         for half in (mine, other):
             ag_arrived(t, half, 0)
             here = normed_half(l, s, half)
@@ -429,16 +430,16 @@
             def rows_of(f, here=here):
                 return jnp.dot(qkvg[l, f], here, preferred_element_type=jnp.float32)
 
-            keys[half] = rows_of(1).astype(jnp.bfloat16)
-            values[half] = rows_of(2).astype(jnp.bfloat16)
+            keys[slot, half] = rows_of(1).astype(jnp.bfloat16)
+            values[slot, half] = rows_of(2).astype(jnp.bfloat16)
             if half is mine:
                 query, gating = rows_of(0).T.astype(jnp.bfloat16), jax.nn.sigmoid(rows_of(3))
                 for b in range(2):
-                    queries[b] = query[b * tokens : (b + 1) * tokens]
-                    gates[b] = gating[:, b * tokens : (b + 1) * tokens]
-
-    def attend(t, last=False):
-        l, s = lax.div(t, group), lax.rem(t, group)
+                    queries[slot, b] = query[b * tokens : (b + 1) * tokens]
+                    gates[slot, b] = gating[:, b * tokens : (b + 1) * tokens]
+
+    def attend(t, blocks=None, kept=False):
+        l, s, slot = lax.div(t, group), lax.rem(t, group), lax.rem(t, 2)
         live = jnp.concatenate([mask_buf[k] for k in range(rows)], axis=1) > 0
         square = lax.broadcasted_iota(jnp.int32, (tokens, tokens), 0) == lax.broadcasted_iota(
             jnp.int32, (tokens, tokens), 1
@@ -446,10 +447,10 @@
 
         def one(h, b):
             at = slice(h * HEAD_DIM, (h + 1) * HEAD_DIM)
-            key_here = jnp.concatenate([keys[k, at] for k in range(2)], axis=1)
-            value_here = jnp.concatenate([values[k, at] for k in range(2)], axis=1)
+            key_here = jnp.concatenate([keys[slot, k, at] for k in range(2)], axis=1)
+            value_here = jnp.concatenate([values[slot, k, at] for k in range(2)], axis=1)
             scores = (
-                jnp.dot(queries[b, :, at], key_here, preferred_element_type=jnp.float32)
+                jnp.dot(queries[slot, b, :, at], key_here, preferred_element_type=jnp.float32)
                 * score_scale
             )
             head_bias = jnp.concatenate([spread[l, b, k, h] for k in range(cols)], axis=1)
@@ -466,14 +467,14 @@
             )
             summed_row = jnp.sum(jnp.where(square, summed, 0.0), axis=0, keepdims=True)
             attended = mixed * (1.0 / summed_row)
-            gated[l, s, b, c, at] = (gates[b, at] * attended).astype(jnp.bfloat16)
-
-        if last:
-            for b in (1 - side, side):
+            gated[l, s, b, c, at] = (gates[slot, b, at] * attended).astype(jnp.bfloat16)
+
+        if blocks is not None:
+            for b in blocks:
                 for h in range(heads):
                     one(h, b)
-                gated_desc(t, 1, b).start()
-                gated_desc(t, 0, b).start()
+                gated_desc(t, 1, b, kept).start()
+                gated_desc(t, 0, b, kept).start()
         else:
             for h in range(heads):
                 for b in range(2):
@@ -481,7 +482,7 @@
             gated_desc(t, 1).start()
             gated_desc(t, 0).start()
 
-    def gated_desc(t, kind, b=None):
+    def gated_desc(t, kind, b=None, kept=False):
         l, s = lax.div(t, group), lax.rem(t, group)
         block = across if kind == 2 else c
         held = gated.at[l, s, :, block] if b is None else gated.at[l, s, b, block]
@@ -489,7 +490,7 @@
             held,
             held,
             gated_sems.at[2, 0, 0],
-            gated_sems.at[kind % 2, 0 if b is None else b, t],
+            gated_sems.at[kind % 2, b if kept else 0, t],
             r,
             across if kind == 1 else sibling,
         )
@@ -512,7 +513,7 @@
     def pass_last(t, b):
         l, s = LAYERS - 1, lax.rem(t, group)
         settle(gated.at[l, s, b, across], gated_sems.at[1, b, t])
-        gated_desc(t, 2, b).start()
+        gated_desc(t, 2, b, True).start()
 
     def finish_last(t, b):
         l, s = LAYERS - 1, lax.rem(t, group)
@@ -549,11 +550,9 @@
             out[side * group + s] = final[s, side]
 
     start_sample(0)
-    for k in range(2, CHUNKS):
-        bias_chunk(k)
-        bias_exchange(0, k)
-        bias_pass(0, k - 2)
-        if k == 2:
+    for k in range(CHUNKS - 2):
+        bias_pass(0, k)
+        if k == 0:
             start_sample(1)
     stage_first(0, mine)
     bias_pass(0, CHUNKS - 2)
@@ -569,44 +568,55 @@
     load(CHUNKS + 7).wait()
     load(CHUNKS + 8).wait()
 
-    forward(0, other)
+    def begin(t, carry):
+        @pl.when(t > 0)
+        def _():
+            forward(t, mine)
+
+        forward(t, other)
+        project(t)
+        attend(t, (side,))
+        return carry
+
+    def complete(t, carry):
+        attend(t, (1 - side,))
+        return carry
+
+    lax.fori_loop(0, 2, begin, 0)
+    bias_arrived(0)
+    for s in range(3, group):
+        start_sample(s)
+    lax.fori_loop(0, 2, complete, 0)
+    stage_first(2, mine)
+    stage_first(2, other)
+    for k in range(CHUNKS // 2):
+        bias_pass(1, k)
+    pass_gated(jnp.int32(0))
+    forward(2, mine)
+    finish(jnp.int32(0))
+    for s in range(3, group):
+        stage_first(s, mine)
+        stage_first(s, other)
+    forward(2, other)
 
     def step(t, carry):
         project(t)
 
-        for k in range(CHUNKS):
-
-            @pl.when(t == max(k, 1))
+        for k in range(CHUNKS // 2, CHUNKS):
+
+            @pl.when(t == min(k, group - 1))
             def _(k=k):
                 bias_pass(1, k)
-
-        @pl.when(t == 0)
-        def _():
-            bias_arrived(0)
 
         @pl.when(t == group)
         def _():
             bias_arrived(1)
 
-        @pl.when(t == 0)
-        def _():
-            for s in range(3, group):
-                start_sample(s)
-
         attend(t)
-
-        @pl.when(t >= 1)
-        def _():
-            pass_gated(t - 1)
-
-        @pl.when(t + 2 < group)
-        def _():
-            stage_first(t + 2, mine)
-            stage_first(t + 2, other)
-
+        pass_gated(t - 1)
         forward(t + 1, mine)
 
-        @pl.when((t >= 1) & (t <= group))
+        @pl.when(t <= group)
         def _():
             finish(t - 1)
 
@@ -619,13 +629,12 @@
             stage_next(t + 2)
 
         forward(t + 1, other)
-
         return carry
 
-    lax.fori_loop(0, tasks - 1, step, 0)
+    lax.fori_loop(2, tasks - 1, step, 0)
     final_task = jnp.int32(tasks - 1)
     project(final_task)
-    attend(final_task, True)
+    attend(final_task, (1 - side, side), True)
     pass_gated(final_task - 1)
     for k in (2, 1):
         finish(final_task - k)
@@ -712,10 +721,10 @@
             pltpu.VMEM((cols, tokens + 16, chans), bf16),
             pltpu.VMEM((width, tokens), f32),
             pltpu.VMEM((rows, 1, tokens), jnp.int32),
-            pltpu.VMEM((2, tokens, width), bf16),
-            pltpu.VMEM((2, width, 2 * tokens), bf16),
-            pltpu.VMEM((2, width, 2 * tokens), bf16),
-            pltpu.VMEM((2, width, tokens), f32),
+            pltpu.VMEM((2, 2, tokens, width), bf16),
+            pltpu.VMEM((2, 2, width, 2 * tokens), bf16),
+            pltpu.VMEM((2, 2, width, 2 * tokens), bf16),
+            pltpu.VMEM((2, 2, width, tokens), f32),
             pltpu.VMEM((LAYERS, group, 2, cols, width, tokens), bf16),
             pltpu.VMEM((group, 2, width, tokens), bf16),
             dma((2,)),

time: 84.6 us -> 83.5 us (0.987)
  Pallas kernels: 82 us -> 80.9 us
    pallas_call x1, Pallas kernels: 82 us -> 80.9 us  [per_device_fused(): pl.pallas_call(lambda *refs: fused(rows, cols, *refs), out_shape=jax.Shap...]
where the time goes in v5:
time: 83.5 us; the launch traced here: 83.3 us
  Pallas kernels  80.9 us (97%)
  local copies, waits for them, and re-layouts  1.77 us (2%)
    pallas_call x1, Pallas kernels, per_device_fused(): pl.pallas_call(lambda *refs: fused(rows, cols, *refs), out_shape=jax.Shap...  80.9 us
    unnamed x1, local copies, waits for them, and re-layouts  1.77 us

profile of v5, /device:TPU:0, one launch (start us, length us, event | category | flops | bytes accessed | tf_op | source)
XLA Modules:
  0.0 83.3 jit_solution(6279491156361605958)
XLA Ops:
  0.7 80.9 %fused_blocks.1 = bf16[8,192,128]{2,1,0:T(8,128)(2,1)} custom-call(bf16[128,128,128]{2,1,0:T(8,128)(2,1)} %refs_0_.1, bf16[32,128]{1,0:T(8,128)(2,1)} %bitcast.13, bf16[8,192,128]{2,1,0:T(8,128)(2,1)} %bitcast.11, bf16[256,128]{1,0:T(8,128)(2,1)} %refs_3_.1, s32[1,256]{1,0:T(1,128)} %bitcast.14, s32[1,1]{1,0:T(1,128)} %bitcast.9.refs_5_, ...), custom_call_target="tpu_custom_call" | custom-call | tf_op jit(solution)/shard_map/fused_blocks/pallas_call | solution.py:701
  81.6 1.8 %copy.13 = bf16[8,128,192]{1,2,0:T(8,128)(2,1)} copy(bf16[8,128,192]{1,2,0:T(8,128)(2,1)} %bitcast.10) | data formatting | bytes 786432

commit v6 on v5

--- a/solution.py
+++ b/solution.py
@@ -438,7 +438,7 @@
                     queries[slot, b] = query[b * tokens : (b + 1) * tokens]
                     gates[slot, b] = gating[:, b * tokens : (b + 1) * tokens]
 
-    def attend(t, blocks=None, kept=False):
+    def attend(t, blocks=None):
         l, s, slot = lax.div(t, group), lax.rem(t, group), lax.rem(t, 2)
         live = jnp.concatenate([mask_buf[k] for k in range(rows)], axis=1) > 0
         square = lax.broadcasted_iota(jnp.int32, (tokens, tokens), 0) == lax.broadcasted_iota(
@@ -470,11 +470,11 @@
             gated[l, s, b, c, at] = (gates[slot, b, at] * attended).astype(jnp.bfloat16)
 
         if blocks is not None:
-            for b in blocks:
+            for i, b in enumerate(blocks):
                 for h in range(heads):
                     one(h, b)
-                gated_desc(t, 1, b, kept).start()
-                gated_desc(t, 0, b, kept).start()
+                gated_desc(t, 1, b, i).start()
+                gated_desc(t, 0, b, i).start()
         else:
             for h in range(heads):
                 for b in range(2):
@@ -482,15 +482,18 @@
             gated_desc(t, 1).start()
             gated_desc(t, 0).start()
 
-    def gated_desc(t, kind, b=None, kept=False):
+    def gated_sem(t, kind, second):
+        return gated_sems.at[2, 1 + kind] if second else gated_sems.at[kind, t]
+
+    def gated_desc(t, kind, b=None, second=0):
         l, s = lax.div(t, group), lax.rem(t, group)
         block = across if kind == 2 else c
         held = gated.at[l, s, :, block] if b is None else gated.at[l, s, b, block]
         return remote(
             held,
             held,
-            gated_sems.at[2, 0, 0],
-            gated_sems.at[kind % 2, b if kept else 0, t],
+            gated_sems.at[2, 0],
+            gated_sem(t, kind % 2, second),
             r,
             across if kind == 1 else sibling,
         )
@@ -507,24 +510,24 @@
 
     def pass_gated(t):
         l, s = lax.div(t, group), lax.rem(t, group)
-        settle(gated.at[l, s, :, across], gated_sems.at[1, 0, t])
+        settle(gated.at[l, s, :, across], gated_sem(t, 1, 0))
         gated_desc(t, 2).start()
 
-    def pass_last(t, b):
+    def pass_last(t, b, second):
         l, s = LAYERS - 1, lax.rem(t, group)
-        settle(gated.at[l, s, b, across], gated_sems.at[1, b, t])
-        gated_desc(t, 2, b, True).start()
-
-    def finish_last(t, b):
+        settle(gated.at[l, s, b, across], gated_sem(t, 1, second))
+        gated_desc(t, 2, b, second).start()
+
+    def finish_last(t, b, second):
         l, s = LAYERS - 1, lax.rem(t, group)
-        settle(gated.at[l, s, b, pl.ds(0, 2)], gated_sems.at[0, b, t])
+        settle(gated.at[l, s, b, pl.ds(0, 2)], gated_sem(t, 0, second))
         joined = jnp.concatenate([gated[l, s, b, k] for k in range(cols)], axis=0)
         update = jnp.dot(out_w[l], joined, preferred_element_type=jnp.float32)
         return (stream[l, s, mine, c, b].astype(jnp.float32) + update).astype(jnp.bfloat16)
 
     def finish(t):
         l, s = lax.div(t, group), lax.rem(t, group)
-        settle(gated.at[l, s, :, pl.ds(0, 2)], gated_sems.at[0, 0, t])
+        settle(gated.at[l, s, :, pl.ds(0, 2)], gated_sem(t, 0, 0))
         joined = jnp.concatenate(
             [
                 jnp.concatenate([gated[l, s, b, k] for k in range(cols)], axis=0)
@@ -550,10 +553,9 @@
             out[side * group + s] = final[s, side]
 
     start_sample(0)
+    start_sample(1)
     for k in range(CHUNKS - 2):
         bias_pass(0, k)
-        if k == 0:
-            start_sample(1)
     stage_first(0, mine)
     bias_pass(0, CHUNKS - 2)
     stage_first(0, other)
@@ -634,15 +636,15 @@
     lax.fori_loop(2, tasks - 1, step, 0)
     final_task = jnp.int32(tasks - 1)
     project(final_task)
-    attend(final_task, (1 - side, side), True)
+    attend(final_task, (1 - side, side))
     pass_gated(final_task - 1)
     for k in (2, 1):
         finish(final_task - k)
-    for b in (1 - side, side):
-        pass_last(final_task, b)
-    final[group - 1, 1 - side] = finish_last(final_task, 1 - side)
+    for i, b in enumerate((1 - side, side)):
+        pass_last(final_task, b, i)
+    final[group - 1, 1 - side] = finish_last(final_task, 1 - side, 0)
     end_desc(group - 1).start()
-    out[side * group + group - 1] = finish_last(final_task, side)
+    out[side * group + group - 1] = finish_last(final_task, side, 1)
 
     settle(out.at[pl.ds((1 - side) * group, group)], end_sems.at[1])
     settle(parts_buf.at[pl.ds(0, cols - 1)], part_sems.at[0])
@@ -652,7 +654,7 @@
         settle(spread.at[l, 0], pair_sems.at[0, l])
     settle(stream.at[0, pl.ds(0, group), 0, pl.ds(0, 3), 0], in_sems.at[2, 0])
     settle(stream.at[1, pl.ds(0, group), 0, 0], swap_sems.at[group])
-    settle(gated.at[:, :, :, pl.ds(0, 3)], gated_sems.at[2, 0, 0])
+    settle(gated.at[:, :, :, pl.ds(0, 3)], gated_sems.at[2, 0])
     settle(out.at[pl.ds(0, group)], end_sems.at[0])
 
     def drain(t, carry):
@@ -734,7 +736,7 @@
             dma((3, group)),
             dma((LAYERS * group, 5)),
             dma((group + 1,)),
-            dma((3, 2, LAYERS * group)),
+            dma((3, LAYERS * group)),
             dma((2,)),
             dma((CHUNKS + 9,)),
         ],

time: 83.5 us -> 83.2 us (level)
  no operation moved by 1% of the time
where the time goes in v6:
time: 83.2 us; the launch traced here: 83 us
  Pallas kernels  80.6 us (97%)
  local copies, waits for them, and re-layouts  1.77 us (2%)
    pallas_call x1, Pallas kernels, per_device_fused(): pl.pallas_call(lambda *refs: fused(rows, cols, *refs), out_shape=jax.Shap...  80.6 us
    unnamed x1, local copies, waits for them, and re-layouts  1.77 us

profile of v6, /device:TPU:0, one launch (start us, length us, event | category | flops | bytes accessed | tf_op | source)
XLA Modules:
  0.0 83.0 jit_solution(11649246034966439736)
XLA Ops:
  0.7 80.6 %fused_blocks.1 = bf16[8,192,128]{2,1,0:T(8,128)(2,1)} custom-call(bf16[128,128,128]{2,1,0:T(8,128)(2,1)} %refs_0_.1, bf16[32,128]{1,0:T(8,128)(2,1)} %bitcast.13, bf16[8,192,128]{2,1,0:T(8,128)(2,1)} %bitcast.11, bf16[256,128]{1,0:T(8,128)(2,1)} %refs_3_.1, s32[1,256]{1,0:T(1,128)} %bitcast.14, s32[1,1]{1,0:T(1,128)} %bitcast.9.refs_5_, ...), custom_call_target="tpu_custom_call" | custom-call | tf_op jit(solution)/shard_map/fused_blocks/pallas_call | solution.py:703
  81.2 1.8 %copy.13 = bf16[8,128,192]{1,2,0:T(8,128)(2,1)} copy(bf16[8,128,192]{1,2,0:T(8,128)(2,1)} %bitcast.10) | data formatting | bytes 786432
